TPU v7x, 128 devices: a whole 4x4x4 slice. The times are simulated.
128 devices in a mesh: space: 16 (over z_lo, y, core), help: 8 (over z_hi, x).
Axes of the slice: x: 4, y: 4, z: 4 (z_hi: 2, z_lo: 2; z = z_hi * 2 + z_lo), core: 2. Of those that a mesh axis runs over, the one named last changes fastest.
Arguments:
- solution: float32 [9, 16384, 512], P(None, ('space', 'help')), may hold values from -6 to 6
- material: float32 [3, 16384, 512], P(None, ('space', 'help')), may hold values from 0.5 to 2
- neighbours: int32 [6, 16384], P(None, ('space', 'help')), may hold values from 0 to 16383, as said below
- refine_count: int32 [16, 8], P('space', 'help'), may hold values from 1 to 64, 256 in all within a row
Outputs:
- evolved: float32 [9, 16384, 512], P(None, ('space', 'help'))
Inputs may be any that keep to these rules, and one draw needn't show every extreme that they name: The neighbours across y and z faces lie on the same device; across x+ on the device next along space (index + 1, wrapping) with the same help index, across x- on the previous one. Neighbours are mutual: the x+ neighbour's x- neighbour is the cell itself, likewise for y and z. `refine_count`: A device's cells whose index within the device is under its count are refined; the counts of one help group sum to 256.
All inputs are finite; a program needn't handle non-finite values.
Results may differ from a plain program's by a relative error of at most 0.0001.
Values sent between devices are 32-bit elements; how exact they have to be, the bound alone decides.
A program may use at most 128 MiB of HBM per device.

v0:
```python
import math

import jax
import jax.numpy as jnp
import ml_dtypes
import numpy as np
from jax import lax
from jax.experimental import pallas as pl
from jax.experimental.pallas import tpu as pltpu
from jax.sharding import PartitionSpec as P

ORD = 8
NODES = 512
PLANE = 64
CELLS = 128
STEP = 0.5
LIFT = 0.5
F32 = jnp.float32
BF16 = jnp.bfloat16
VMEM_LIMIT = 40 * 2**20

COLS = {6: 0, 7: 1, 8: 2, 4: 3, 3: 4, 1: 5, 5: 6, 2: 7}
X_FIELDS = (6, 7, 8, 0, 3, 5)


def cheb_table(node_count):
    intervals = node_count - 1
    places = np.arange(node_count)
    points = np.cos(np.pi * places / intervals)
    weights = np.where((places == 0) | (places == intervals), 2.0, 1.0)
    scaled = weights * (-1.0) ** places
    differ = points[:, None] - points[None, :] + np.eye(node_count)
    matrix = np.outer(scaled, 1.0 / scaled) / differ
    matrix = matrix - np.eye(node_count) * np.sum(matrix, axis=1)[:, None]
    return matrix / (node_count * node_count / 4.0)


TABLE = cheb_table(8)
EVEN = [[float((TABLE[i, j] + TABLE[i, 7 - j]) / 2) for j in range(4)] for i in range(4)]
ODD = [[float((TABLE[i, j] - TABLE[i, 7 - j]) / 2) for j in range(4)] for i in range(4)]


def plane_table():
    both = np.concatenate([np.kron(TABLE, np.eye(8)), np.kron(np.eye(8), TABLE)])
    both = both.astype(np.float32)
    high = both.astype(ml_dtypes.bfloat16)
    low = (both - high.astype(np.float32)).astype(ml_dtypes.bfloat16)
    return np.concatenate([high, high, low], axis=1)


def weight(degree):
    return STEP ** (degree + 1) / math.factorial(degree + 1)


def line_derivative(lines):
    plus = [lines[j] + lines[7 - j] for j in range(4)]
    minus = [lines[j] - lines[7 - j] for j in range(4)]
    out = [None] * 8
    for i in range(4):
        first = EVEN[i][0] * plus[0]
        second = ODD[i][0] * minus[0]
        for j in range(1, 4):
            first = first + EVEN[i][j] * plus[j]
            second = second + ODD[i][j] * minus[j]
        out[i] = second + first
        out[7 - i] = second - first
    return out


def rows(start, size):
    if isinstance(start, int):
        return pl.ds(start, size)
    return pl.ds(pl.multiple_of(start, 8), size)


def put_operand(r_ref, a, field, value):
    high = value.astype(BF16)
    low = (value - high.astype(F32)).astype(BF16)
    column = pl.ds(COLS[field] * CELLS, CELLS)
    base = a * 192
    if not isinstance(a, int):
        base = pl.multiple_of(base, 16)
    r_ref[pl.ds(base, 64), column] = high
    r_ref[pl.ds(base + 64, 64), column] = low
    r_ref[pl.ds(base + 128, 64), column] = high


def slopes(q_ref, r_ref, k_ref, t_ref, x_ref):
    def body(i, carry):
        base = pl.multiple_of(i * 192, 16)
        r = r_ref[pl.ds(base, 192), :]
        k = k_ref[...]
        both = jnp.dot(k, r[:, :512], preferred_element_type=F32)
        along_y = jnp.dot(k[:64], r[:, 512:768], preferred_element_type=F32)
        along_z = jnp.dot(k[64:], r[:, 768:], preferred_element_type=F32)

        def put(slot, value):
            t_ref[rows(slot * NODES + i * PLANE, PLANE), :] = value

        put(0, both[:64, 128:256])
        put(1, both[64:, 256:384])
        put(2, both[:64, :128])
        put(3, both[64:, 128:256] + both[:64, 256:384])
        put(4, both[64:, :128])
        put(5, along_y[:, :128] + along_z[:, :128])
        put(6, along_y[:, 128:] + both[64:, 384:])
        put(7, both[:64, 384:] + along_z[:, 128:])
        for slot, field in enumerate(X_FIELDS):
            lines = [q_ref[rows(field * NODES + a * PLANE + i * 8, 8), :] for a in range(8)]
            for a, value in enumerate(line_derivative(lines)):
                x_ref[rows(slot * NODES + a * PLANE + i * 8, 8), :] = value
        return carry

    lax.fori_loop(0, 8, body, 0)


def elastic_plane(a, t_ref, x_ref, m_ref):
    def t(slot):
        return t_ref[rows(slot * NODES + a * PLANE, PLANE), :]

    def x(slot):
        return x_ref[rows(slot * NODES + a * PLANE, PLANE), :]

    def m(slot):
        return m_ref[rows(slot * NODES + a * PLANE, PLANE), :]

    lam, shear, inverse = m(0), m(1), m(2)
    twice = shear + shear
    xx, yy, zz = x(0), t(0), t(1)
    spread = lam * (xx + yy + zz)
    return [
        spread + twice * xx,
        spread + twice * yy,
        spread + twice * zz,
        shear * (t(2) + x(1)),
        shear * t(3),
        shear * (t(4) + x(2)),
        inverse * (x(3) + t(5)),
        inverse * (x(4) + t(6)),
        inverse * (x(5) + t(7)),
    ]


def predict_kernel(
    sol_ref, mat_ref, count_ref, w_ref, k_ref,
    q0_ref, i_ref, m_ref, low_ref, high_ref, mface_ref,
    q_ref, r_ref, t_ref, x_ref,
):
    for field in range(9):
        for tile in range(4):
            block = sol_ref[field, :, tile * 128 : (tile + 1) * 128].T
            at = pl.ds(field * NODES + tile * 128, 128)
            q0_ref[at, :] = block
            q_ref[at, :] = block
            if field in COLS:
                put_operand(r_ref, 2 * tile, field, block[:64])
                put_operand(r_ref, 2 * tile + 1, field, block[64:])
    for tile in range(4):
        span = slice(tile * 128, (tile + 1) * 128)
        density = mat_ref[0, :, span].T
        lam = mat_ref[1, :, span].T
        shear = mat_ref[2, :, span].T
        inverse = 1.0 / density
        for slot, value in enumerate(
            (lam, shear, inverse, jnp.sqrt((lam + 2.0 * shear) / density))
        ):
            m_ref[pl.ds(slot * NODES + tile * 128, 128), :] = value

    slopes(q_ref, r_ref, k_ref, t_ref, x_ref)

    def first(a, carry):
        for field, value in enumerate(elastic_plane(a, t_ref, x_ref, m_ref)):
            at = rows(field * NODES + a * PLANE, PLANE)
            i_ref[at, :] = weight(0) * q0_ref[at, :] + weight(1) * value
            q_ref[at, :] = value
            if field in COLS:
                put_operand(r_ref, a, field, value)
        return carry

    lax.fori_loop(0, 8, first, 0)
    refined = lax.broadcasted_iota(jnp.int32, (8, CELLS), 1) < count_ref[0, 0]

    def term(degree, carry):
        slopes(q_ref, r_ref, k_ref, t_ref, x_ref)
        share = jnp.where(refined, w_ref[degree], 0.0)[None]

        def later(a, inner):
            for field, value in enumerate(elastic_plane(a, t_ref, x_ref, m_ref)):
                at = rows(field * NODES + a * PLANE, PLANE)
                added = (value.reshape(8, 8, CELLS) * share).reshape(PLANE, CELLS)
                i_ref[at, :] = i_ref[at, :] + added
                q_ref[at, :] = value
                if field in COLS:
                    put_operand(r_ref, a, field, value)
            return inner

        lax.fori_loop(0, 8, later, 0)
        return carry

    lax.fori_loop(2, ORD, term, 0)
    for out_ref, a in ((low_ref, 0), (high_ref, 7)):
        for field in range(9):
            out_ref[pl.ds(field * PLANE, PLANE), :] = i_ref[pl.ds(field * NODES + a * PLANE, PLANE), :]
        out_ref[pl.ds(9 * PLANE, PLANE), :] = m_ref[pl.ds(3 * NODES + a * PLANE, PLANE), :]
    for side, a in enumerate((0, 7)):
        for slot in range(3):
            mface_ref[pl.ds((side * 3 + slot) * PLANE, PLANE), :] = m_ref[
                pl.ds(slot * NODES + a * PLANE, PLANE), :
            ]


def fetch(far, targets):
    high = far.astype(BF16)
    low = (far - high.astype(F32)).astype(BF16)
    picks = (
        lax.broadcasted_iota(jnp.int32, (CELLS, CELLS), 0) == jnp.broadcast_to(targets, (CELLS, CELLS))
    ).astype(F32).astype(BF16)
    return jnp.dot(
        jnp.concatenate([high, low], axis=1),
        jnp.concatenate([picks, picks], axis=0),
        preferred_element_type=F32,
    )


def flux(own, far, lam, shear, inverse, direction, sign):
    jump = [far[f] - own[f] for f in range(9)]
    top = jnp.maximum(own[9], far[9]) * (0.5 * LIFT)
    scale = 0.5 * LIFT * sign
    lam, shear, inverse = lam * scale, shear * scale, inverse * scale
    normal = {0: 6, 1: 7, 2: 8}[direction]
    stress = {0: (0, 3, 5), 1: (3, 1, 4), 2: (5, 4, 2)}[direction]
    out = [top * jump[f] for f in range(9)]
    across = lam * jump[normal]
    for f in range(3):
        out[f] = out[f] + across
    out[direction] = out[direction] + 2.0 * shear * jump[normal]
    for other in range(3):
        if other != direction:
            slot = {(0, 1): 3, (1, 2): 4, (0, 2): 5}[(min(direction, other), max(direction, other))]
            out[slot] = out[slot] + shear * jump[6 + other]
    for other in range(3):
        out[6 + other] = out[6 + other] + inverse * jump[stress[other]]
    return out


def correct_kernel(i_ref, q0_ref, m_ref, n_ref, k_ref, e_ref, r_ref, t_ref, x_ref, far_ref):
    def split(a, carry):
        for field in COLS:
            put_operand(r_ref, a, field, i_ref[rows(field * NODES + a * PLANE, PLANE), :])
        return carry

    lax.fori_loop(0, 8, split, 0)
    slopes(i_ref, r_ref, k_ref, t_ref, x_ref)

    def volume(a, carry):
        for field, value in enumerate(elastic_plane(a, t_ref, x_ref, m_ref)):
            at = rows(field * NODES + a * PLANE, PLANE)
            e_ref[at, :] = q0_ref[at, :] + value
        return carry

    lax.fori_loop(0, 8, volume, 0)

    def y_face(ref, slot, place):
        return [ref[pl.ds(slot * NODES + a * PLANE + place * 8, 8), :] for a in range(8)]

    def z_face(ref, slot, place):
        return ref[pl.ds(slot * NODES + place, PLANE, stride=8), :]

    for face in (2, 3):
        own_place, far_place, sign = (0, 7, 1.0) if face % 2 else (7, 0, -1.0)
        targets = n_ref[pl.ds(face, 1), :] & (CELLS - 1)
        far = jnp.concatenate(
            [x for f in range(9) for x in y_face(i_ref, f, far_place)] + y_face(m_ref, 3, far_place), axis=0
        )
        far_ref[...] = fetch(far, targets)
        for a in range(8):
            at = a * PLANE + own_place * 8

            def pick(ref, slot):
                return ref[pl.ds(slot * NODES + at, 8), :]

            own = [pick(i_ref, f) for f in range(9)] + [pick(m_ref, 3)]
            other = [far_ref[pl.ds(f * PLANE + a * 8, 8), :] for f in range(10)]
            for f, value in enumerate(
                flux(own, other, pick(m_ref, 0), pick(m_ref, 1), pick(m_ref, 2), 1, sign)
            ):
                e_ref[pl.ds(f * NODES + at, 8), :] = pick(e_ref, f) + value
    for face in (4, 5):
        own_place, far_place, sign = (0, 7, 1.0) if face % 2 else (7, 0, -1.0)
        targets = n_ref[pl.ds(face, 1), :] & (CELLS - 1)
        far = jnp.concatenate(
            [z_face(i_ref, f, far_place) for f in range(9)] + [z_face(m_ref, 3, far_place)], axis=0
        )
        got = fetch(far, targets)
        own = [z_face(i_ref, f, own_place) for f in range(9)] + [z_face(m_ref, 3, own_place)]
        other = [got[f * PLANE : (f + 1) * PLANE] for f in range(10)]
        for f, value in enumerate(
            flux(own, other, z_face(m_ref, 0, own_place), z_face(m_ref, 1, own_place), z_face(m_ref, 2, own_place), 2, sign)
        ):
            e_ref[pl.ds(f * NODES + own_place, PLANE, stride=8), :] = z_face(e_ref, f, own_place) + value


def finish_kernel(e_ref, low_ref, high_ref, mface_ref, before_ref, after_ref, n_ref, out_ref, x_ref):
    for face, far_ref, own_ref, side, sign in ((0, before_ref, high_ref, 1, -1.0), (1, after_ref, low_ref, 0, 1.0)):
        got = fetch(far_ref[...], n_ref[pl.ds(face, 1), :] & (CELLS - 1))
        own = [own_ref[pl.ds(f * PLANE, PLANE), :] for f in range(10)]
        other = [got[f * PLANE : (f + 1) * PLANE] for f in range(10)]
        lam, shear, inverse = (mface_ref[pl.ds((side * 3 + s) * PLANE, PLANE), :] for s in range(3))
        for f, value in enumerate(flux(own, other, lam, shear, inverse, 0, sign)):
            x_ref[pl.ds((side * 9 + f) * PLANE, PLANE), :] = value
    for field in range(9):
        for tile in range(4):
            block = e_ref[pl.ds(field * NODES + tile * 128, 128), :]
            if tile == 0:
                block = jnp.concatenate([block[:64] + x_ref[pl.ds(field * PLANE, PLANE), :], block[64:]], axis=0)
            if tile == 3:
                block = jnp.concatenate(
                    [block[:64], block[64:] + x_ref[pl.ds((9 + field) * PLANE, PLANE), :]], axis=0
                )
            out_ref[field, :, tile * 128 : (tile + 1) * 128] = block.T


def shifted(value, axis, by):
    peers = lax.axis_size(axis)
    return lax.ppermute(value, axis, [(i, (i + by) % peers) for i in range(peers)])


def shape(*dims):
    return jax.ShapeDtypeStruct(dims, F32)


def whole():
    return pl.BlockSpec(memory_space=pltpu.VMEM)


def predict(solution, material, refine_count):
    table = jnp.asarray(plane_table())
    weights = jnp.asarray([weight(k) for k in range(ORD)], F32)
    smem = pl.BlockSpec(memory_space=pltpu.SMEM)
    return pl.pallas_call(
        predict_kernel,
        out_shape=(
            shape(9 * NODES, CELLS),
            shape(9 * NODES, CELLS),
            shape(4 * NODES, CELLS),
            shape(10 * PLANE, CELLS),
            shape(10 * PLANE, CELLS),
            shape(6 * PLANE, CELLS),
        ),
        in_specs=[whole(), whole(), smem, smem, whole()],
        out_specs=[whole()] * 6,
        scratch_shapes=[
            pltpu.VMEM((9 * NODES, CELLS), F32),
            pltpu.VMEM((8 * 192, 8 * CELLS), BF16),
            pltpu.VMEM((8 * NODES, CELLS), F32),
            pltpu.VMEM((6 * NODES, CELLS), F32),
        ],
        compiler_params=pltpu.CompilerParams(vmem_limit_bytes=VMEM_LIMIT),
        name="predict",
    )(solution, material, refine_count, weights, table)


def correct(integral, start, mats, neighbours):
    table = jnp.asarray(plane_table())
    return pl.pallas_call(
        correct_kernel,
        out_shape=shape(9 * NODES, CELLS),
        in_specs=[whole()] * 5,
        out_specs=whole(),
        scratch_shapes=[
            pltpu.VMEM((8 * 192, 8 * CELLS), BF16),
            pltpu.VMEM((8 * NODES, CELLS), F32),
            pltpu.VMEM((6 * NODES, CELLS), F32),
            pltpu.VMEM((10 * PLANE, CELLS), F32),
        ],
        compiler_params=pltpu.CompilerParams(vmem_limit_bytes=VMEM_LIMIT),
        cost_estimate=pl.CostEstimate(flops=8_000_000_000, bytes_accessed=30_000_000, transcendentals=0),
        name="correct",
    )(integral, start, mats, neighbours, table)


def finish(partial, low, high, mface, before, after, neighbours):
    return pl.pallas_call(
        finish_kernel,
        out_shape=shape(9, CELLS, NODES),
        in_specs=[whole()] * 7,
        out_specs=whole(),
        scratch_shapes=[pltpu.VMEM((18 * PLANE, CELLS), F32)],
        compiler_params=pltpu.CompilerParams(vmem_limit_bytes=VMEM_LIMIT),
        name="finish",
    )(partial, low, high, mface, before, after, neighbours)


def on_device(solution, material, neighbours, refine_count):
    start, integral, mats, low, high, mface = predict(solution, material, refine_count)
    after = shifted(high, "space", -1)
    before = shifted(low, "space", 1)
    partial = correct(integral, start, mats, neighbours)
    return finish(partial, low, high, mface, before, after, neighbours)


def solution(mesh):
    in_specs = (
        P(None, ("space", "help"), None),
        P(None, ("space", "help"), None),
        P(None, ("space", "help")),
        P("space", "help"),
    )
    out_specs = P(None, ("space", "help"), None)
    return jax.shard_map(
        on_device, mesh=mesh, in_specs=in_specs, out_specs=out_specs, check_vma=False
    )
```

profile of v0, /device:TPU:25, one launch (start us, length us, event | category | flops | bytes accessed | tf_op | source)
XLA Modules:
  0.0 44.7 jit_solution(10356561017621400513)
XLA Ops:
  0.7 0.0 copy-start
  0.7 1.7 %copy-done = f32[9,128,512]{2,1,0:T(8,128)S(1)} copy-done((f32[9,128,512]{2,1,0:T(8,128)S(1)}, f32[9,128,512]{2,1,0:T(8,128)}, u32[]{:S(2)}) %copy-start) | copy-done | bytes 2359320
  2.3 0.0 copy-start.1
  2.3 1.1 %copy-done.1 = f32[3,128,512]{2,1,0:T(8,128)S(1)} copy-done((f32[3,128,512]{2,1,0:T(8,128)S(1)}, f32[3,128,512]{2,1,0:T(8,128)}, u32[]{:S(2)}) %copy-start.1) | copy-done | bytes 786456
  3.5 0.0 copy-start.2
  3.5 0.8 %copy-done.2 = bf16[128,192]{1,0:T(8,128)(2,1)S(1)} copy-done((bf16[128,192]{1,0:T(8,128)(2,1)S(1)}, bf16[128,192]{1,0:T(8,128)(2,1)}, u32[]{:S(2)}) %copy-start.2) | copy-done | bytes 49176
  4.3 0.0 copy-start.5
  4.3 0.7 %copy-done.5 = f32[8]{0:T(128)S(1)} copy-done((f32[8]{0:T(128)S(1)}, f32[8]{0:T(128)}, u32[]{:S(2)}) %copy-start.5) | copy-done | bytes 56
  4.9 0.0 copy-start.3
  5.0 0.0 copy-start.4
  5.0 27.0 %predict.1 = (f32[4608,128]{1,0:T(8,128)S(1)}, f32[4608,128]{1,0:T(8,128)S(1)}, f32[2048,128]{1,0:T(8,128)S(1)}, f32[640,128]{1,0:T(8,128)S(1)}, f32[640,128]{1,0:T(8,128)S(1)}, /*index=5*/f32[384,128]{1,0:T(8,128)S(1)}) custom-call(f32[9,128,512]{2,1,0:T(8,128)S(1)} %copy-done, f32[3,128,512]{2,1,0:T(8,128)S(1)} %copy-done.1, s32[1,1]{1,0:T(1,128)S(6)} %copy.8.count_ref, ...), custom_call_target="tpu_custom_call" | custom-call | tf_op jit(solution)/shard_map/predict/pallas_call | solution.py:340
  31.9 1.9 %collective-permute-start = (f32[640,128]{1,0:T(8,128)S(1)}, f32[640,128]{1,0:T(8,128)S(1)}, u32[]{:S(2)}, u32[]{:S(2)}) collective-permute-start(f32[640,128]{1,0:T(8,128)S(1)} %get-tuple-element.14.low_ref), channel_id=1, source_target_pairs={{0,8},{8,16},{16,24},{24,32},{32,40},{40,48},{48,56},{56,64},{64,7... | collective-permute-start | bytes 983048 | tf_op jit(solution)/shard_map/ppermute | solution.py:325
  33.8 0.0 collective-permute-start.1
  33.8 0.0 copy-done.3
  33.8 0.0 copy-done.4
  33.9 4.5 %correct.1.e_ref = f32[4608,128]{1,0:T(8,128)S(1)} custom-call(f32[4608,128]{1,0:T(8,128)S(1)} %get-tuple-element.11.i_ref, f32[4608,128]{1,0:T(8,128)S(1)} %get-tuple-element.12.q0_ref, f32[2048,128]{1,0:T(8,128)S(1)} %get-tuple-element.13.m_ref, s32[6,128]{1,0:T(8,128)S(1)} %copy-done.4, bf16[128,192]{1,0:T(8,128)(2,1)S(1)} %copy-done.3), custom_call_target="tpu_custom_call" | custom-call | flops 8000000000 | bytes 30000000 | tf_op jit(solution)/shard_map/correct/pallas_call | solution.py:365
  38.3 0.0 collective-permute-done.before_ref
  38.4 4.1 %collective-permute-done.1.after_ref = f32[640,128]{1,0:T(8,128)S(1)} collective-permute-done((f32[640,128]{1,0:T(8,128)S(1)}, f32[640,128]{1,0:T(8,128)S(1)}, u32[]{:S(2)}, u32[]{:S(2)}) %collective-permute-start.1) | collective-permute-done | bytes 327712 | tf_op jit(solution)/shard_map/ppermute | solution.py:325
  42.5 2.3 %finish.1 = f32[9,128,512]{2,1,0:T(8,128)} custom-call(f32[4608,128]{1,0:T(8,128)S(1)} %correct.1.e_ref, f32[640,128]{1,0:T(8,128)S(1)} %get-tuple-element.14.low_ref, f32[640,128]{1,0:T(8,128)S(1)} %get-tuple-element.15.high_ref, f32[384,128]{1,0:T(8,128)S(1)} %get-tuple-element.16.mface_ref, f32[640,128]{1,0:T(8,128)S(1)} %collective-permute-done.before_ref, ...), custom_call_target="tpu_custom_call" | custom-call | tf_op jit(solution)/shard_map/finish/pallas_call | solution.py:383
Async XLA Ops:
  0.7 1.7 %copy-start = (f32[9,128,512]{2,1,0:T(8,128)S(1)}, f32[9,128,512]{2,1,0:T(8,128)}, u32[]{:S(2)}) copy-start(f32[9,128,512]{2,1,0:T(8,128)} %sol_ref.1) | copy-start | bytes 7077892
  2.3 1.1 %copy-start.1 = (f32[3,128,512]{2,1,0:T(8,128)S(1)}, f32[3,128,512]{2,1,0:T(8,128)}, u32[]{:S(2)}) copy-start(f32[3,128,512]{2,1,0:T(8,128)} %mat_ref.1) | copy-start | bytes 2359300
  3.5 0.8 %copy-start.2 = (bf16[128,192]{1,0:T(8,128)(2,1)S(1)}, bf16[128,192]{1,0:T(8,128)(2,1)}, u32[]{:S(2)}) copy-start(bf16[128,192]{1,0:T(8,128)(2,1)} %constant.4.clone.k_ref) | copy-start | bytes 147460
  4.3 0.7 %copy-start.5 = (f32[8]{0:T(128)S(1)}, f32[8]{0:T(128)}, u32[]{:S(2)}) copy-start(f32[8]{0:T(128)} %constant.5.clone.w_ref) | copy-start | bytes 100
  4.9 28.9 %copy-start.3 = (bf16[128,192]{1,0:T(8,128)(2,1)S(1)}, bf16[128,192]{1,0:T(8,128)(2,1)}, u32[]{:S(2)}) copy-start(bf16[128,192]{1,0:T(8,128)(2,1)} %constant.4.clone.k_ref) | copy-start | bytes 147460
  5.0 28.9 %copy-start.4 = (s32[6,128]{1,0:T(8,128)S(1)}, s32[6,128]{1,0:T(8,128)}, u32[]{:S(2)}) copy-start(s32[6,128]{1,0:T(8,128)} %n_ref.3) | copy-start | bytes 9220
  31.9 6.4 %collective-permute-start = (f32[640,128]{1,0:T(8,128)S(1)}, f32[640,128]{1,0:T(8,128)S(1)}, u32[]{:S(2)}, u32[]{:S(2)}) collective-permute-start(f32[640,128]{1,0:T(8,128)S(1)} %get-tuple-element.14.low_ref), channel_id=1, source_target_pairs={{0,8},{8,16},{16,24},{24,32},{32,40},{40,48},{48,56},{56,64},{64,7... | collective-permute-start | bytes 983048 | tf_op jit(solution)/shard_map/ppermute | solution.py:325
  33.8 8.6 %collective-permute-start.1 = (f32[640,128]{1,0:T(8,128)S(1)}, f32[640,128]{1,0:T(8,128)S(1)}, u32[]{:S(2)}, u32[]{:S(2)}) collective-permute-start(f32[640,128]{1,0:T(8,128)S(1)} %get-tuple-element.15.high_ref), channel_id=1, source_target_pairs={{0,120},{8,0},{16,8},{24,16},{32,24},{40,32},{48,40},{56,48},{64,5... | collective-permute-start | bytes 983048 | tf_op jit(solution)/shard_map/ppermute | solution.py:325
where the time goes:
time: 45 us; the launch traced here: 44.7 us
  Pallas kernels  33.7 us (75%)
  local copies, waits for them, and re-layouts  4.29 us (10%)
  waiting for transfers between devices  4.1 us (9%)
  starting transfers between devices  1.93 us (4%)
  between operations  0.69 us (2%)
    pallas_call x1, Pallas kernels, predict(): pl.pallas_call(predict_kernel, out_shape=(shape(9 * NODES, CELLS), shape(...  27 us
    pallas_call x1, Pallas kernels, correct(): pl.pallas_call(correct_kernel, out_shape=shape(9 * NODES, CELLS), in_spec...  4.49 us
    unnamed x12, local copies, waits for them, and re-layouts  4.29 us
    ppermute x2, waiting for transfers between devices, shifted(): lax.ppermute(value, axis, [(i, (i + by) % peers) for i in range(peers)])  4.1 us
    pallas_call x1, Pallas kernels, finish(): pl.pallas_call(finish_kernel, out_shape=shape(9, CELLS, NODES), in_specs=...  2.27 us
    ppermute x2, starting transfers between devices, shifted(): lax.ppermute(value, axis, [(i, (i + by) % peers) for i in range(peers)])  1.93 us
  transfers between devices with their start and end apart: 2, of which 1 were waited for; matrix products, arithmetic and copies ran while one was open for 0% of the time, Pallas kernels for 10%

commit v1 on v0

v1 whole, which is shorter than its diff:
```python
import math

import jax
import jax.numpy as jnp
import ml_dtypes
import numpy as np
from jax import lax
from jax.experimental import pallas as pl
from jax.experimental.pallas import tpu as pltpu
from jax.sharding import PartitionSpec as P

ORD = 8
NODES = 512
PLANE = 64
CELLS = 128
STEP = 0.5
LIFT = 0.5
F32 = jnp.float32
BF16 = jnp.bfloat16
VMEM_LIMIT = 40 * 2**20

COLS = (6, 7, 8, 4, 3, 1, 5, 2)
X_FIELDS = (6, 7, 8, 0, 3, 5)


def cheb_table(node_count):
    intervals = node_count - 1
    places = np.arange(node_count)
    points = np.cos(np.pi * places / intervals)
    weights = np.where((places == 0) | (places == intervals), 2.0, 1.0)
    scaled = weights * (-1.0) ** places
    differ = points[:, None] - points[None, :] + np.eye(node_count)
    matrix = np.outer(scaled, 1.0 / scaled) / differ
    matrix = matrix - np.eye(node_count) * np.sum(matrix, axis=1)[:, None]
    return matrix / (node_count * node_count / 4.0)


TABLE = cheb_table(8)
EVEN = [[float((TABLE[i, j] + TABLE[i, 7 - j]) / 2) for j in range(4)] for i in range(4)]
ODD = [[float((TABLE[i, j] - TABLE[i, 7 - j]) / 2) for j in range(4)] for i in range(4)]


def plane_table():
    both = np.concatenate([np.kron(TABLE, np.eye(8)), np.kron(np.eye(8), TABLE)])
    both = both.astype(np.float32)
    high = both.astype(ml_dtypes.bfloat16).astype(np.float32)
    low = (both - high).astype(ml_dtypes.bfloat16).astype(np.float32)
    return np.concatenate([high, high, low, np.zeros_like(low)], axis=1)


def weight(degree):
    return STEP ** (degree + 1) / math.factorial(degree + 1)


def line_derivative(lines):
    plus = [lines[j] + lines[7 - j] for j in range(4)]
    minus = [lines[j] - lines[7 - j] for j in range(4)]
    out = [None] * 8
    for i in range(4):
        first = EVEN[i][0] * plus[0]
        second = ODD[i][0] * minus[0]
        for j in range(1, 4):
            first = first + EVEN[i][j] * plus[j]
            second = second + ODD[i][j] * minus[j]
        out[i] = second + first
        out[7 - i] = second - first
    return out


def swap(value):
    return pltpu.roll(value, 64, axis=1)


def pair_derivative(lines, c_ref):
    sign = c_ref[pl.ds(128, 8), :]
    parts = [swap(v) + sign * v for v in lines]
    out = []
    for i in range(4):
        total = c_ref[pl.ds(i * 32, 8), :] * parts[0]
        for j in range(1, 4):
            total = total + c_ref[pl.ds(i * 32 + j * 8, 8), :] * parts[j]
        out.append(total + sign * swap(total))
    return out


def fill_pair_table(c_ref):
    lower = lax.broadcasted_iota(jnp.int32, (8, CELLS), 1) < 64
    for i in range(4):
        for j in range(4):
            c_ref[pl.ds(i * 32 + j * 8, 8), :] = jnp.where(lower, EVEN[i][j], ODD[i][j])
    c_ref[pl.ds(128, 8), :] = jnp.where(lower, 1.0, -1.0)


def plane(ref, slot, a, planes):
    return ref[pl.ds((slot * planes + a) * PLANE, PLANE), :]


def halves(value):
    high = value.astype(BF16)
    low = (value - high.astype(F32)).astype(BF16)
    return high, low


def slopes(q_ref, k_ref, t_ref, x_ref, planes, c_ref=None):
    k = k_ref[...].astype(BF16)[:, :192]

    def lines(b):
        for slot, field in enumerate(X_FIELDS):
            at = [pl.ds((field * planes + a) * PLANE + b * 8, 8) for a in range(planes)]
            values = [q_ref[place, :] for place in at]
            values = line_derivative(values) if c_ref is None else pair_derivative(values, c_ref)
            for a, value in enumerate(values):
                x_ref[pl.ds((slot * planes + a) * PLANE + b * 8, 8), :] = value

    for i in range(planes):
        split = {}
        for field in COLS:
            high, low = halves(plane(q_ref, field, i, planes))
            split[field] = jnp.concatenate([high, low, high], axis=0)

        def dot(left, fields):
            right = jnp.concatenate([split[f] for f in fields], axis=1)
            return jnp.dot(left, right, preferred_element_type=F32)

        both = dot(k, (6, 7, 8, 4))
        along_y = dot(k[:64], (3, 1))
        along_z = dot(k[64:], (5, 2))
        step = 8 // planes
        for b in range(i * step, (i + 1) * step):
            lines(b)

        def put(slot, value):
            t_ref[pl.ds((slot * planes + i) * PLANE, PLANE), :] = value

        put(0, both[:64, 128:256])
        put(1, both[64:, 256:384])
        put(2, both[:64, :128])
        put(3, both[64:, 128:256] + both[:64, 256:384])
        put(4, both[64:, :128])
        put(5, along_y[:, :128] + along_z[:, :128])
        put(6, along_y[:, 128:] + both[64:, 384:])
        put(7, both[:64, 384:] + along_z[:, 128:])


def elastic_plane(a, t_ref, x_ref, m_ref, planes, scale=None):
    def t(slot):
        return plane(t_ref, slot, a, planes)

    def x(slot):
        return plane(x_ref, slot, a, planes)

    lam, shear, inverse = (plane(m_ref, slot, a, planes) for slot in range(3))
    if scale is not None:
        lam, shear, inverse = lam * scale, shear * scale, inverse * scale
    twice = shear + shear
    xx, yy, zz = x(0), t(0), t(1)
    spread = lam * (xx + yy + zz)
    return [
        spread + twice * xx,
        spread + twice * yy,
        spread + twice * zz,
        shear * (t(2) + x(1)),
        shear * t(3),
        shear * (t(4) + x(2)),
        inverse * (x(3) + t(5)),
        inverse * (x(4) + t(6)),
        inverse * (x(5) + t(7)),
    ]


def predict_kernel(
    sol_hbm, mat_hbm, count_ref, k_hbm,
    q0_ref, i_ref, m_ref, low_ref, high_ref, mface_ref, k_ref,
    sol_ref, mat_ref, q_ref, u_ref, p_ref, t_ref, x_ref, c_ref, sem,
):
    copies = [pltpu.make_async_copy(sol_hbm.at[f], sol_ref.at[f], sem.at[f]) for f in range(9)]
    copies.append(pltpu.make_async_copy(mat_hbm, mat_ref, sem.at[9]))
    copies.append(pltpu.make_async_copy(k_hbm, k_ref, sem.at[10]))
    for copy in copies:
        copy.start()
    fill_pair_table(c_ref)
    for field in range(9):
        copies[field].wait()
        for tile in range(4):
            q0_ref[pl.ds(field * NODES + tile * 128, 128), :] = sol_ref[field, :, tile * 128 : (tile + 1) * 128].T
    copies[9].wait()
    copies[10].wait()
    for tile in range(4):
        span = slice(tile * 128, (tile + 1) * 128)
        density = mat_ref[0, :, span].T
        lam = mat_ref[1, :, span].T
        shear = mat_ref[2, :, span].T
        inverse = 1.0 / density
        for slot, value in enumerate(
            (lam, shear, inverse, jnp.sqrt((lam + 2.0 * shear) / density))
        ):
            m_ref[pl.ds(slot * NODES + tile * 128, 128), :] = value
    lower = lax.broadcasted_iota(jnp.int32, (PLANE, CELLS), 1) < 64

    def packed(first, second):
        return jnp.where(lower, first, swap(second))

    for slot in range(3):
        for j in range(4):
            p_ref[pl.ds((slot * 4 + j) * PLANE, PLANE), :] = packed(
                plane(m_ref, slot, j, 8), plane(m_ref, slot, 7 - j, 8)
            )

    slopes(q0_ref, k_ref, t_ref, x_ref, 8)
    for j in range(4):
        sides = [elastic_plane(a, t_ref, x_ref, m_ref, 8) for a in (j, 7 - j)]
        for field in range(9):
            for a, side in ((j, sides[0]), (7 - j, sides[1])):
                i_ref[pl.ds((field * 8 + a) * PLANE, PLANE), :] = (
                    weight(0) * plane(q0_ref, field, a, 8) + weight(1) * side[field]
                )
            value = packed(sides[0][field], sides[1][field])
            q_ref[pl.ds((field * 4 + j) * PLANE, PLANE), :] = value
            u_ref[pl.ds((field * 4 + j) * PLANE, PLANE), :] = value

    def nested(turn, scale):
        slopes(u_ref, k_ref, t_ref, x_ref, 4, c_ref)
        for j in range(4):
            for field, value in enumerate(elastic_plane(j, t_ref, x_ref, p_ref, 4, scale)):
                u_ref[pl.ds((field * 4 + j) * PLANE, PLANE), :] = plane(q_ref, field, j, 4) + value
        degree = (7 - turn).astype(F32)
        return scale * ((degree + 1.0) / degree)

    lax.fori_loop(0, ORD - 3, nested, jnp.float32(STEP / ORD))
    slopes(u_ref, k_ref, t_ref, x_ref, 4, c_ref)
    refined = lax.broadcasted_iota(jnp.int32, (PLANE, CELLS), 1) < count_ref[0, 0]
    for j in range(4):
        for field, value in enumerate(elastic_plane(j, t_ref, x_ref, p_ref, 4, weight(2))):
            for a, part in ((j, value), (7 - j, swap(value))):
                at = pl.ds((field * 8 + a) * PLANE, PLANE)
                i_ref[at, :] = i_ref[at, :] + jnp.where(refined, part, 0.0)

    for out_ref, a in ((low_ref, 0), (high_ref, 7)):
        for field in range(9):
            out_ref[pl.ds(field * PLANE, PLANE), :] = plane(i_ref, field, a, 8)
        out_ref[pl.ds(9 * PLANE, PLANE), :] = plane(m_ref, 3, a, 8)
    for side, a in enumerate((0, 7)):
        for slot in range(3):
            mface_ref[pl.ds((side * 3 + slot) * PLANE, PLANE), :] = plane(m_ref, slot, a, 8)


def fetch(far, targets):
    high = far.astype(BF16)
    low = (far - high.astype(F32)).astype(BF16)
    picks = (
        lax.broadcasted_iota(jnp.int32, (CELLS, CELLS), 0) == jnp.broadcast_to(targets, (CELLS, CELLS))
    ).astype(F32).astype(BF16)
    return jnp.dot(
        jnp.concatenate([high, low], axis=1),
        jnp.concatenate([picks, picks], axis=0),
        preferred_element_type=F32,
    )


def flux(own, far, lam, shear, inverse, direction, sign):
    jump = [far[f] - own[f] for f in range(9)]
    top = jnp.maximum(own[9], far[9]) * (0.5 * LIFT)
    scale = 0.5 * LIFT * sign
    lam, shear, inverse = lam * scale, shear * scale, inverse * scale
    normal = {0: 6, 1: 7, 2: 8}[direction]
    stress = {0: (0, 3, 5), 1: (3, 1, 4), 2: (5, 4, 2)}[direction]
    out = [top * jump[f] for f in range(9)]
    across = lam * jump[normal]
    for f in range(3):
        out[f] = out[f] + across
    out[direction] = out[direction] + 2.0 * shear * jump[normal]
    for other in range(3):
        if other != direction:
            slot = {(0, 1): 3, (1, 2): 4, (0, 2): 5}[(min(direction, other), max(direction, other))]
            out[slot] = out[slot] + shear * jump[6 + other]
    for other in range(3):
        out[6 + other] = out[6 + other] + inverse * jump[stress[other]]
    return out


def correct_kernel(i_ref, q0_ref, m_ref, n_ref, k_ref, e_ref, t_ref, x_ref, far_ref):
    slopes(i_ref, k_ref, t_ref, x_ref, 8)
    for a in range(8):
        for field, value in enumerate(elastic_plane(a, t_ref, x_ref, m_ref, 8)):
            at = pl.ds(field * NODES + a * PLANE, PLANE)
            e_ref[at, :] = q0_ref[at, :] + value

    def y_face(ref, slot, place):
        return [ref[pl.ds(slot * NODES + a * PLANE + place * 8, 8), :] for a in range(8)]

    def z_face(ref, slot, place):
        return ref[pl.ds(slot * NODES + place, PLANE, stride=8), :]

    for face in (2, 3):
        own_place, far_place, sign = (0, 7, 1.0) if face % 2 else (7, 0, -1.0)
        targets = n_ref[pl.ds(face, 1), :] & (CELLS - 1)
        far = jnp.concatenate(
            [x for f in range(9) for x in y_face(i_ref, f, far_place)] + y_face(m_ref, 3, far_place), axis=0
        )
        far_ref[...] = fetch(far, targets)
        for a in range(8):
            at = a * PLANE + own_place * 8

            def pick(ref, slot):
                return ref[pl.ds(slot * NODES + at, 8), :]

            own = [pick(i_ref, f) for f in range(9)] + [pick(m_ref, 3)]
            other = [far_ref[pl.ds(f * PLANE + a * 8, 8), :] for f in range(10)]
            for f, value in enumerate(
                flux(own, other, pick(m_ref, 0), pick(m_ref, 1), pick(m_ref, 2), 1, sign)
            ):
                e_ref[pl.ds(f * NODES + at, 8), :] = pick(e_ref, f) + value
    for face in (4, 5):
        own_place, far_place, sign = (0, 7, 1.0) if face % 2 else (7, 0, -1.0)
        targets = n_ref[pl.ds(face, 1), :] & (CELLS - 1)
        far = jnp.concatenate(
            [z_face(i_ref, f, far_place) for f in range(9)] + [z_face(m_ref, 3, far_place)], axis=0
        )
        got = fetch(far, targets)
        own = [z_face(i_ref, f, own_place) for f in range(9)] + [z_face(m_ref, 3, own_place)]
        other = [got[f * PLANE : (f + 1) * PLANE] for f in range(10)]
        for f, value in enumerate(
            flux(own, other, z_face(m_ref, 0, own_place), z_face(m_ref, 1, own_place), z_face(m_ref, 2, own_place), 2, sign)
        ):
            e_ref[pl.ds(f * NODES + own_place, PLANE, stride=8), :] = z_face(e_ref, f, own_place) + value


def finish_kernel(e_ref, low_ref, high_ref, mface_ref, before_ref, after_ref, n_ref, out_ref, x_ref):
    @pl.when(pl.program_id(0) == 0)
    def _():
        for face, far_ref, own_ref, side, sign in (
            (0, before_ref, high_ref, 1, -1.0),
            (1, after_ref, low_ref, 0, 1.0),
        ):
            got = fetch(far_ref[...], n_ref[pl.ds(face, 1), :] & (CELLS - 1))
            own = [own_ref[pl.ds(f * PLANE, PLANE), :] for f in range(10)]
            other = [got[f * PLANE : (f + 1) * PLANE] for f in range(10)]
            lam, shear, inverse = (mface_ref[pl.ds((side * 3 + s) * PLANE, PLANE), :] for s in range(3))
            for f, value in enumerate(flux(own, other, lam, shear, inverse, 0, sign)):
                x_ref[pl.ds((side * 9 + f) * PLANE, PLANE), :] = value

    base = pl.program_id(0) * 3
    for part in range(3):
        field = base + part
        for tile in range(4):
            block = e_ref[pl.ds(pl.multiple_of(field * NODES + tile * 128, 128), 128), :]
            low = x_ref[pl.ds(pl.multiple_of(field * PLANE, PLANE), PLANE), :]
            high = x_ref[pl.ds(pl.multiple_of((9 + field) * PLANE, PLANE), PLANE), :]
            if tile == 0:
                block = jnp.concatenate([block[:64] + low, block[64:]], axis=0)
            if tile == 3:
                block = jnp.concatenate([block[:64], block[64:] + high], axis=0)
            out_ref[part, :, tile * 128 : (tile + 1) * 128] = block.T


def shifted(value, axis, by):
    peers = lax.axis_size(axis)
    return lax.ppermute(value, axis, [(i, (i + by) % peers) for i in range(peers)])


def shape(*dims):
    return jax.ShapeDtypeStruct(dims, F32)


def whole():
    return pl.BlockSpec(memory_space=pltpu.VMEM)


def predict(solution, material, refine_count):
    table = jnp.asarray(plane_table())
    smem = pl.BlockSpec(memory_space=pltpu.SMEM)
    hbm = pl.BlockSpec(memory_space=pltpu.MemorySpace.HBM)
    return pl.pallas_call(
        predict_kernel,
        out_shape=(
            shape(9 * NODES, CELLS),
            shape(9 * NODES, CELLS),
            shape(4 * NODES, CELLS),
            shape(10 * PLANE, CELLS),
            shape(10 * PLANE, CELLS),
            shape(6 * PLANE, CELLS),
            shape(128, 256),
        ),
        in_specs=[hbm, hbm, smem, hbm],
        out_specs=[whole()] * 7,
        scratch_shapes=[
            pltpu.VMEM((9, CELLS, NODES), F32),
            pltpu.VMEM((3, CELLS, NODES), F32),
            pltpu.VMEM((9 * NODES // 2, CELLS), F32),
            pltpu.VMEM((9 * NODES // 2, CELLS), F32),
            pltpu.VMEM((3 * NODES // 2, CELLS), F32),
            pltpu.VMEM((8 * NODES, CELLS), F32),
            pltpu.VMEM((6 * NODES, CELLS), F32),
            pltpu.VMEM((136, CELLS), F32),
            pltpu.SemaphoreType.DMA((11,)),
        ],
        compiler_params=pltpu.CompilerParams(vmem_limit_bytes=VMEM_LIMIT),
        name="predict",
    )(solution, material, refine_count, table)


def correct(integral, start, mats, neighbours, table):
    return pl.pallas_call(
        correct_kernel,
        out_shape=shape(9 * NODES, CELLS),
        in_specs=[whole()] * 5,
        out_specs=whole(),
        scratch_shapes=[
            pltpu.VMEM((8 * NODES, CELLS), F32),
            pltpu.VMEM((6 * NODES, CELLS), F32),
            pltpu.VMEM((10 * PLANE, CELLS), F32),
        ],
        compiler_params=pltpu.CompilerParams(vmem_limit_bytes=VMEM_LIMIT),
        cost_estimate=pl.CostEstimate(flops=8_000_000_000, bytes_accessed=30_000_000, transcendentals=0),
        name="correct",
    )(integral, start, mats, neighbours, table)


def finish(partial, low, high, mface, before, after, neighbours):
    return pl.pallas_call(
        finish_kernel,
        out_shape=shape(9, CELLS, NODES),
        grid=(3,),
        in_specs=[whole()] * 7,
        out_specs=pl.BlockSpec((3, CELLS, NODES), lambda i: (i, 0, 0)),
        scratch_shapes=[pltpu.VMEM((18 * PLANE, CELLS), F32)],
        compiler_params=pltpu.CompilerParams(vmem_limit_bytes=VMEM_LIMIT),
        name="finish",
    )(partial, low, high, mface, before, after, neighbours)


def on_device(solution, material, neighbours, refine_count):
    start, integral, mats, low, high, mface, table = predict(solution, material, refine_count)
    after = shifted(high, "space", -1)
    before = shifted(low, "space", 1)
    partial = correct(integral, start, mats, neighbours, table)
    return finish(partial, low, high, mface, before, after, neighbours)


def solution(mesh):
    in_specs = (
        P(None, ("space", "help"), None),
        P(None, ("space", "help"), None),
        P(None, ("space", "help")),
        P("space", "help"),
    )
    out_specs = P(None, ("space", "help"), None)
    return jax.shard_map(
        on_device, mesh=mesh, in_specs=in_specs, out_specs=out_specs, check_vma=False
    )
```

time: 45 us -> 38.9 us (0.86)
  the two profiles are of different devices: /device:TPU:25 before, /device:TPU:29 now
where the time goes in v1:
time: 38.9 us; the launch traced here: 38.7 us
  Pallas kernels  26.3 us (68%)
  waiting for transfers between devices  6.09 us (16%)
  local copies, waits for them, and re-layouts  3.7 us (10%)
  starting transfers between devices  1.94 us (5%)
  between operations  0.68 us (2%)
    pallas_call x1, Pallas kernels, predict(): pl.pallas_call(predict_kernel, out_shape=(shape(9 * NODES, CELLS), shape(...  21 us
    ppermute x2, waiting for transfers between devices, shifted(): lax.ppermute(value, axis, [(i, (i + by) % peers) for i in range(peers)])  6.09 us
    unnamed x8, local copies, waits for them, and re-layouts  3.7 us
    pallas_call x1, Pallas kernels, finish(): pl.pallas_call(finish_kernel, out_shape=shape(9, CELLS, NODES), grid=(3,)...  2.75 us
    pallas_call x1, Pallas kernels, correct(): pl.pallas_call(correct_kernel, out_shape=shape(9 * NODES, CELLS), in_spec...  2.51 us
    ppermute x2, starting transfers between devices, shifted(): lax.ppermute(value, axis, [(i, (i + by) % peers) for i in range(peers)])  1.94 us
  transfers between devices with their start and end apart: 2, of which 2 were waited for; matrix products, arithmetic and copies ran while one was open for 0% of the time, Pallas kernels for 6%

profile of v1, /device:TPU:29, one launch (start us, length us, event | category | flops | bytes accessed | tf_op | source)
XLA Modules:
  0.0 38.7 jit_solution(1260333165740857305)
XLA Ops:
  0.7 0.0 copy-start
  0.7 1.7 %copy-done = f32[9,128,512]{2,1,0:T(8,128)S(1)} copy-done((f32[9,128,512]{2,1,0:T(8,128)S(1)}, f32[9,128,512]{2,1,0:T(8,128)}, u32[]{:S(2)}) %copy-start) | copy-done | bytes 2359320
  2.3 0.0 copy-start.1
  2.3 1.1 %copy-done.1 = f32[3,128,512]{2,1,0:T(8,128)S(1)} copy-done((f32[3,128,512]{2,1,0:T(8,128)S(1)}, f32[3,128,512]{2,1,0:T(8,128)}, u32[]{:S(2)}) %copy-start.1) | copy-done | bytes 786456
  3.5 0.0 copy-start.2
  3.5 0.9 %copy-done.2 = f32[128,256]{1,0:T(8,128)S(1)} copy-done((f32[128,256]{1,0:T(8,128)S(1)}, f32[128,256]{1,0:T(8,128)}, u32[]{:S(2)}) %copy-start.2) | copy-done | bytes 131096
  4.4 0.0 copy-start.3
  4.4 21.0 %predict.1 = (f32[4608,128]{1,0:T(8,128)S(1)}, f32[4608,128]{1,0:T(8,128)S(1)}, f32[2048,128]{1,0:T(8,128)S(1)}, f32[640,128]{1,0:T(8,128)S(1)}, f32[640,128]{1,...) custom-call(f32[9,128,512]{2,1,0:T(8,128)S(1)} %copy-done, f32[3,128,512]{2,1,0:T(8,128)S(1)} %copy-done.1, ...), custom_call_target="tpu_custom_call" | custom-call | tf_op jit(solution)/shard_map/predict/pallas_call | solution.py:373
  25.4 1.9 %collective-permute-start = (f32[640,128]{1,0:T(8,128)S(1)}, f32[640,128]{1,0:T(8,128)S(1)}, u32[]{:S(2)}, u32[]{:S(2)}) collective-permute-start(f32[640,128]{1,0:T(8,128)S(1)} %get-tuple-element.16.low_ref), channel_id=1, source_target_pairs={{0,8},{8,16},{16,24},{24,32},{32,40},{40,48},{48,56},{56,64},{64,7... | collective-permute-start | bytes 983048 | tf_op jit(solution)/shard_map/ppermute | solution.py:358
  27.3 0.0 collective-permute-start.1
  27.3 0.0 copy-done.3
  27.3 2.5 %correct.1.e_ref = f32[4608,128]{1,0:T(8,128)S(1)} custom-call(f32[4608,128]{1,0:T(8,128)S(1)} %get-tuple-element.12.i_ref, f32[4608,128]{1,0:T(8,128)S(1)} %get-tuple-element.13.q0_ref, f32[2048,128]{1,0:T(8,128)S(1)} %get-tuple-element.14.m_ref, s32[6,128]{1,0:T(8,128)S(1)} %copy-done.3, f32[128,256]{1,0:T(8,128)S(1)} %get-tuple-element.15.k_ref), custom_call_target="tpu_custom_call" | custom-call | flops 8000000000 | bytes 30000000 | tf_op jit(solution)/shard_map/correct/pallas_call | solution.py:403
  29.9 1.5 %collective-permute-done.before_ref = f32[640,128]{1,0:T(8,128)S(1)} collective-permute-done((f32[640,128]{1,0:T(8,128)S(1)}, f32[640,128]{1,0:T(8,128)S(1)}, u32[]{:S(2)}, u32[]{:S(2)}) %collective-permute-start) | collective-permute-done | bytes 327712 | tf_op jit(solution)/shard_map/ppermute | solution.py:358
  31.3 4.6 %collective-permute-done.1.after_ref = f32[640,128]{1,0:T(8,128)S(1)} collective-permute-done((f32[640,128]{1,0:T(8,128)S(1)}, f32[640,128]{1,0:T(8,128)S(1)}, u32[]{:S(2)}, u32[]{:S(2)}) %collective-permute-start.1) | collective-permute-done | bytes 327712 | tf_op jit(solution)/shard_map/ppermute | solution.py:358
  35.9 2.8 %finish.1 = f32[9,128,512]{2,1,0:T(8,128)} custom-call(f32[4608,128]{1,0:T(8,128)S(1)} %correct.1.e_ref, f32[640,128]{1,0:T(8,128)S(1)} %get-tuple-element.16.low_ref, f32[640,128]{1,0:T(8,128)S(1)} %get-tuple-element.17.high_ref, f32[384,128]{1,0:T(8,128)S(1)} %get-tuple-element.18.mface_ref, f32[640,128]{1,0:T(8,128)S(1)} %collective-permute-done.before_ref, ...), custom_call_target="tpu_custom_call" | custom-call | tf_op jit(solution)/shard_map/finish/pallas_call | solution.py:420
Async XLA Ops:
  0.7 1.7 %copy-start = (f32[9,128,512]{2,1,0:T(8,128)S(1)}, f32[9,128,512]{2,1,0:T(8,128)}, u32[]{:S(2)}) copy-start(f32[9,128,512]{2,1,0:T(8,128)} %sol_hbm.1) | copy-start | bytes 7077892
  2.3 1.1 %copy-start.1 = (f32[3,128,512]{2,1,0:T(8,128)S(1)}, f32[3,128,512]{2,1,0:T(8,128)}, u32[]{:S(2)}) copy-start(f32[3,128,512]{2,1,0:T(8,128)} %mat_hbm.1) | copy-start | bytes 2359300
  3.5 0.9 %copy-start.2 = (f32[128,256]{1,0:T(8,128)S(1)}, f32[128,256]{1,0:T(8,128)}, u32[]{:S(2)}) copy-start(f32[128,256]{1,0:T(8,128)} %constant.2.clone.k_hbm) | copy-start | bytes 393220
  4.4 23.0 %copy-start.3 = (s32[6,128]{1,0:T(8,128)S(1)}, s32[6,128]{1,0:T(8,128)}, u32[]{:S(2)}) copy-start(s32[6,128]{1,0:T(8,128)} %n_ref.3) | copy-start | bytes 9220
  25.4 6.0 %collective-permute-start = (f32[640,128]{1,0:T(8,128)S(1)}, f32[640,128]{1,0:T(8,128)S(1)}, u32[]{:S(2)}, u32[]{:S(2)}) collective-permute-start(f32[640,128]{1,0:T(8,128)S(1)} %get-tuple-element.16.low_ref), channel_id=1, source_target_pairs={{0,8},{8,16},{16,24},{24,32},{32,40},{40,48},{48,56},{56,64},{64,7... | collective-permute-start | bytes 983048 | tf_op jit(solution)/shard_map/ppermute | solution.py:358
  27.3 8.6 %collective-permute-start.1 = (f32[640,128]{1,0:T(8,128)S(1)}, f32[640,128]{1,0:T(8,128)S(1)}, u32[]{:S(2)}, u32[]{:S(2)}) collective-permute-start(f32[640,128]{1,0:T(8,128)S(1)} %get-tuple-element.17.high_ref), channel_id=1, source_target_pairs={{0,120},{8,0},{16,8},{24,16},{32,24},{40,32},{48,40},{56,48},{64,5... | collective-permute-start | bytes 983048 | tf_op jit(solution)/shard_map/ppermute | solution.py:358

commit v2 on v1

v2 whole, which is shorter than its diff:
```python
import math

import jax
import jax.numpy as jnp
import ml_dtypes
import numpy as np
from jax import lax
from jax.experimental import pallas as pl
from jax.experimental.pallas import tpu as pltpu
from jax.sharding import PartitionSpec as P

ORD = 8
NODES = 512
PLANE = 64
CELLS = 128
STEP = 0.5
LIFT = 0.5
F32 = jnp.float32
BF16 = jnp.bfloat16
VMEM_LIMIT = 61 * 2**20

COLS = (6, 7, 8, 4, 3, 1, 5, 2)
X_FIELDS = (6, 7, 8, 0, 3, 5)


def cheb_table(node_count):
    intervals = node_count - 1
    places = np.arange(node_count)
    points = np.cos(np.pi * places / intervals)
    weights = np.where((places == 0) | (places == intervals), 2.0, 1.0)
    scaled = weights * (-1.0) ** places
    differ = points[:, None] - points[None, :] + np.eye(node_count)
    matrix = np.outer(scaled, 1.0 / scaled) / differ
    matrix = matrix - np.eye(node_count) * np.sum(matrix, axis=1)[:, None]
    return matrix / (node_count * node_count / 4.0)


TABLE = cheb_table(8)
EVEN = [[float((TABLE[i, j] + TABLE[i, 7 - j]) / 2) for j in range(4)] for i in range(4)]
ODD = [[float((TABLE[i, j] - TABLE[i, 7 - j]) / 2) for j in range(4)] for i in range(4)]


def plane_table():
    both = np.concatenate([np.kron(TABLE, np.eye(8)), np.kron(np.eye(8), TABLE)])
    both = both.astype(np.float32)
    high = both.astype(ml_dtypes.bfloat16).astype(np.float32)
    low = (both - high).astype(ml_dtypes.bfloat16).astype(np.float32)
    return np.concatenate([high, high, low, np.zeros_like(low)], axis=1)


def weight(degree):
    return STEP ** (degree + 1) / math.factorial(degree + 1)


def line_derivative(lines):
    plus = [lines[j] + lines[7 - j] for j in range(4)]
    minus = [lines[j] - lines[7 - j] for j in range(4)]
    out = [None] * 8
    for i in range(4):
        first = EVEN[i][0] * plus[0]
        second = ODD[i][0] * minus[0]
        for j in range(1, 4):
            first = first + EVEN[i][j] * plus[j]
            second = second + ODD[i][j] * minus[j]
        out[i] = second + first
        out[7 - i] = second - first
    return out


def plane(ref, slot, a):
    return ref[pl.ds(slot * NODES + a * PLANE, PLANE), :]


def halves(value):
    high = value.astype(BF16)
    low = (value - high.astype(F32)).astype(BF16)
    return high, low


def slopes(q_ref, k_ref, t_ref, x_ref):
    k = k_ref[...].astype(BF16)[:, :192]

    for i in range(8):
        split = {}
        for field in COLS:
            high, low = halves(plane(q_ref, field, i))
            split[field] = jnp.concatenate([high, low, high], axis=0)

        def dot(left, fields):
            right = jnp.concatenate([split[f] for f in fields], axis=1)
            return jnp.dot(left, right, preferred_element_type=F32)

        both = dot(k, (6, 7, 8, 4))
        along_y = dot(k[:64], (3, 1))
        along_z = dot(k[64:], (5, 2))
        for slot, field in enumerate(X_FIELDS):
            lines = [q_ref[pl.ds(field * NODES + a * PLANE + i * 8, 8), :] for a in range(8)]
            for a, value in enumerate(line_derivative(lines)):
                x_ref[pl.ds(slot * NODES + a * PLANE + i * 8, 8), :] = value

        def put(slot, value):
            t_ref[pl.ds(slot * NODES + i * PLANE, PLANE), :] = value

        put(0, both[:64, 128:256])
        put(1, both[64:, 256:384])
        put(2, both[:64, :128])
        put(3, both[64:, 128:256] + both[:64, 256:384])
        put(4, both[64:, :128])
        put(5, along_y[:, :128] + along_z[:, :128])
        put(6, along_y[:, 128:] + both[64:, 384:])
        put(7, both[:64, 384:] + along_z[:, 128:])


def elastic_plane(a, t_ref, x_ref, m_ref, scale=None):
    def t(slot):
        return plane(t_ref, slot, a)

    def x(slot):
        return plane(x_ref, slot, a)

    lam, shear, inverse = (plane(m_ref, slot, a) for slot in range(3))
    if scale is not None:
        lam, shear, inverse = lam * scale, shear * scale, inverse * scale
    twice = shear + shear
    xx, yy, zz = x(0), t(0), t(1)
    spread = lam * (xx + yy + zz)
    return [
        spread + twice * xx,
        spread + twice * yy,
        spread + twice * zz,
        shear * (t(2) + x(1)),
        shear * t(3),
        shear * (t(4) + x(2)),
        inverse * (x(3) + t(5)),
        inverse * (x(4) + t(6)),
        inverse * (x(5) + t(7)),
    ]


def remote(src, dst, send, recv, peer):
    return pltpu.make_async_remote_copy(
        src_ref=src,
        dst_ref=dst,
        send_sem=send,
        recv_sem=recv,
        device_id={"space": peer},
        device_id_type=pl.DeviceIdType.MESH,
    )


def step_kernel(
    sol_hbm, mat_hbm, n_hbm, count_ref, k_hbm,
    e_hbm,
    sol_ref, mat_ref, n_ref, k_ref, q0_ref, q_ref, u_ref, i_ref, m_ref, t_ref, x_ref, far_ref,
    e_ref, before_ref, after_ref, low_ref, high_ref,
    sem, send_sem, recv_sem, out_sem,
):
    me = lax.axis_index("space")
    peers = lax.axis_size("space")
    right, left = lax.rem(me + 1, peers), lax.rem(me + peers - 1, peers)
    barrier = pltpu.get_barrier_semaphore()
    for peer in (left, right):
        pl.semaphore_signal(barrier, inc=1, device_id={"space": peer}, device_id_type=pl.DeviceIdType.MESH)

    copies = [pltpu.make_async_copy(sol_hbm.at[f], sol_ref.at[f], sem.at[f]) for f in range(9)]
    copies.append(pltpu.make_async_copy(mat_hbm, mat_ref, sem.at[9]))
    copies.append(pltpu.make_async_copy(k_hbm, k_ref, sem.at[10]))
    copies.append(pltpu.make_async_copy(n_hbm, n_ref, sem.at[11]))
    for copy in copies:
        copy.start()
    for field in range(9):
        copies[field].wait()
        for tile in range(4):
            q0_ref[pl.ds(field * NODES + tile * 128, 128), :] = sol_ref[field, :, tile * 128 : (tile + 1) * 128].T
    for copy in copies[9:]:
        copy.wait()
    for tile in range(4):
        span = slice(tile * 128, (tile + 1) * 128)
        density = mat_ref[0, :, span].T
        lam = mat_ref[1, :, span].T
        shear = mat_ref[2, :, span].T
        inverse = 1.0 / density
        for slot, value in enumerate(
            (lam, shear, inverse, jnp.sqrt((lam + 2.0 * shear) / density))
        ):
            m_ref[pl.ds(slot * NODES + tile * 128, 128), :] = value

    slopes(q0_ref, k_ref, t_ref, x_ref)
    for a in range(8):
        for field, value in enumerate(elastic_plane(a, t_ref, x_ref, m_ref)):
            at = pl.ds(field * NODES + a * PLANE, PLANE)
            i_ref[at, :] = weight(0) * plane(q0_ref, field, a) + weight(1) * value
            q_ref[at, :] = value
            u_ref[at, :] = value

    def nested(turn, scale):
        slopes(u_ref, k_ref, t_ref, x_ref)
        for a in range(8):
            for field, value in enumerate(elastic_plane(a, t_ref, x_ref, m_ref, scale)):
                u_ref[pl.ds(field * NODES + a * PLANE, PLANE), :] = plane(q_ref, field, a) + value
        degree = (7 - turn).astype(F32)
        return scale * ((degree + 1.0) / degree)

    lax.fori_loop(0, ORD - 3, nested, jnp.float32(STEP / ORD))
    slopes(u_ref, k_ref, t_ref, x_ref)
    refined = lax.broadcasted_iota(jnp.int32, (PLANE, CELLS), 1) < count_ref[0, 0]
    for a in range(8):
        for field, value in enumerate(elastic_plane(a, t_ref, x_ref, m_ref, weight(2))):
            at = pl.ds(field * NODES + a * PLANE, PLANE)
            i_ref[at, :] = i_ref[at, :] + jnp.where(refined, value, 0.0)

    for out_ref, a in ((low_ref, 0), (high_ref, 7)):
        for field in range(9):
            out_ref[pl.ds(field * PLANE, PLANE), :] = plane(i_ref, field, a)
        out_ref[pl.ds(9 * PLANE, PLANE), :] = plane(m_ref, 3, a)
    pl.semaphore_wait(barrier, 2)
    sends = [
        remote(low_ref, before_ref, send_sem.at[0], recv_sem.at[0], right),
        remote(high_ref, after_ref, send_sem.at[1], recv_sem.at[1], left),
    ]
    for send in sends:
        send.start()
    volume_and_faces(i_ref, q0_ref, m_ref, n_ref, k_ref, e_ref, t_ref, x_ref, far_ref)

    def writing(field, a, planes, slot):
        at = pl.ds(field * NODES + a * PLANE, planes * PLANE)
        return pltpu.make_async_copy(e_ref.at[at], e_hbm.at[at], out_sem.at[slot * 9 + field])

    writes = [writing(field, 1, 6, 0) for field in range(9)]
    for write in writes:
        write.start()
    for send in sends:
        send.wait()
    for face, far_ref, a, sign in ((0, before_ref, 7, -1.0), (1, after_ref, 0, 1.0)):
        got = fetch(far_ref[...], n_ref[pl.ds(face, 1), :] & (CELLS - 1))
        own = [plane(i_ref, f, a) for f in range(9)] + [plane(m_ref, 3, a)]
        other = [got[f * PLANE : (f + 1) * PLANE] for f in range(10)]
        lam, shear, inverse = (plane(m_ref, slot, a) for slot in range(3))
        for f, value in enumerate(flux(own, other, lam, shear, inverse, 0, sign)):
            e_ref[pl.ds(f * NODES + a * PLANE, PLANE), :] = plane(e_ref, f, a) + value
        for field in range(9):
            writes.append(writing(field, a, 1, 1 + face))
            writes[-1].start()
    for write in writes:
        write.wait()


def fetch(far, targets):
    high = far.astype(BF16)
    low = (far - high.astype(F32)).astype(BF16)
    picks = (
        lax.broadcasted_iota(jnp.int32, (CELLS, CELLS), 0) == jnp.broadcast_to(targets, (CELLS, CELLS))
    ).astype(F32).astype(BF16)
    return jnp.dot(
        jnp.concatenate([high, low], axis=1),
        jnp.concatenate([picks, picks], axis=0),
        preferred_element_type=F32,
    )


def flux(own, far, lam, shear, inverse, direction, sign):
    jump = [far[f] - own[f] for f in range(9)]
    top = jnp.maximum(own[9], far[9]) * (0.5 * LIFT)
    scale = 0.5 * LIFT * sign
    lam, shear, inverse = lam * scale, shear * scale, inverse * scale
    normal = {0: 6, 1: 7, 2: 8}[direction]
    stress = {0: (0, 3, 5), 1: (3, 1, 4), 2: (5, 4, 2)}[direction]
    out = [top * jump[f] for f in range(9)]
    across = lam * jump[normal]
    for f in range(3):
        out[f] = out[f] + across
    out[direction] = out[direction] + 2.0 * shear * jump[normal]
    for other in range(3):
        if other != direction:
            slot = {(0, 1): 3, (1, 2): 4, (0, 2): 5}[(min(direction, other), max(direction, other))]
            out[slot] = out[slot] + shear * jump[6 + other]
    for other in range(3):
        out[6 + other] = out[6 + other] + inverse * jump[stress[other]]
    return out


def volume_and_faces(i_ref, q0_ref, m_ref, n_ref, k_ref, e_ref, t_ref, x_ref, far_ref):
    slopes(i_ref, k_ref, t_ref, x_ref)
    for a in range(8):
        for field, value in enumerate(elastic_plane(a, t_ref, x_ref, m_ref)):
            at = pl.ds(field * NODES + a * PLANE, PLANE)
            e_ref[at, :] = q0_ref[at, :] + value

    def y_face(ref, slot, place):
        return [ref[pl.ds(slot * NODES + a * PLANE + place * 8, 8), :] for a in range(8)]

    def z_face(ref, slot, place):
        return ref[pl.ds(slot * NODES + place, PLANE, stride=8), :]

    for face in (2, 3):
        own_place, far_place, sign = (0, 7, 1.0) if face % 2 else (7, 0, -1.0)
        targets = n_ref[pl.ds(face, 1), :] & (CELLS - 1)
        far = jnp.concatenate(
            [x for f in range(9) for x in y_face(i_ref, f, far_place)] + y_face(m_ref, 3, far_place), axis=0
        )
        far_ref[...] = fetch(far, targets)
        for a in range(8):
            at = a * PLANE + own_place * 8

            def pick(ref, slot):
                return ref[pl.ds(slot * NODES + at, 8), :]

            own = [pick(i_ref, f) for f in range(9)] + [pick(m_ref, 3)]
            other = [far_ref[pl.ds(f * PLANE + a * 8, 8), :] for f in range(10)]
            for f, value in enumerate(
                flux(own, other, pick(m_ref, 0), pick(m_ref, 1), pick(m_ref, 2), 1, sign)
            ):
                e_ref[pl.ds(f * NODES + at, 8), :] = pick(e_ref, f) + value
    for face in (4, 5):
        own_place, far_place, sign = (0, 7, 1.0) if face % 2 else (7, 0, -1.0)
        targets = n_ref[pl.ds(face, 1), :] & (CELLS - 1)
        far = jnp.concatenate(
            [z_face(i_ref, f, far_place) for f in range(9)] + [z_face(m_ref, 3, far_place)], axis=0
        )
        got = fetch(far, targets)
        own = [z_face(i_ref, f, own_place) for f in range(9)] + [z_face(m_ref, 3, own_place)]
        other = [got[f * PLANE : (f + 1) * PLANE] for f in range(10)]
        for f, value in enumerate(
            flux(own, other, z_face(m_ref, 0, own_place), z_face(m_ref, 1, own_place), z_face(m_ref, 2, own_place), 2, sign)
        ):
            e_ref[pl.ds(f * NODES + own_place, PLANE, stride=8), :] = z_face(e_ref, f, own_place) + value


def finish_kernel(e_ref, out_ref):
    for tile in range(4):
        out_ref[0, :, tile * 128 : (tile + 1) * 128] = e_ref[tile * 128 : (tile + 1) * 128, :].T


def shape(*dims):
    return jax.ShapeDtypeStruct(dims, F32)


def step(solution, material, neighbours, refine_count):
    table = jnp.asarray(plane_table())
    smem = pl.BlockSpec(memory_space=pltpu.SMEM)
    hbm = pl.BlockSpec(memory_space=pltpu.MemorySpace.HBM)

    def field_buffer(count):
        return pltpu.VMEM((count * NODES, CELLS), F32)

    return pl.pallas_call(
        step_kernel,
        out_shape=shape(9 * NODES, CELLS),
        in_specs=[hbm, hbm, hbm, smem, hbm],
        out_specs=hbm,
        scratch_shapes=[
            pltpu.VMEM((9, CELLS, NODES), F32),
            pltpu.VMEM((3, CELLS, NODES), F32),
            pltpu.VMEM((6, CELLS), jnp.int32),
            pltpu.VMEM((128, 256), F32),
            field_buffer(9),
            field_buffer(9),
            field_buffer(9),
            field_buffer(9),
            field_buffer(4),
            field_buffer(8),
            field_buffer(6),
            pltpu.VMEM((10 * PLANE, CELLS), F32),
            field_buffer(9),
            pltpu.VMEM((10 * PLANE, CELLS), F32),
            pltpu.VMEM((10 * PLANE, CELLS), F32),
            pltpu.VMEM((10 * PLANE, CELLS), F32),
            pltpu.VMEM((10 * PLANE, CELLS), F32),
            pltpu.SemaphoreType.DMA((12,)),
            pltpu.SemaphoreType.DMA((2,)),
            pltpu.SemaphoreType.DMA((2,)),
            pltpu.SemaphoreType.DMA((27,)),
        ],
        compiler_params=pltpu.CompilerParams(
            vmem_limit_bytes=VMEM_LIMIT, collective_id=0, has_side_effects=True
        ),
        name="step",
    )(solution, material, neighbours, refine_count, table)


def finish(nodal):
    return pl.pallas_call(
        finish_kernel,
        out_shape=shape(9, CELLS, NODES),
        grid=(9,),
        in_specs=[pl.BlockSpec((NODES, CELLS), lambda i: (i, 0))],
        out_specs=pl.BlockSpec((1, CELLS, NODES), lambda i: (i, 0, 0)),
        compiler_params=pltpu.CompilerParams(vmem_limit_bytes=VMEM_LIMIT),
        name="finish",
    )(nodal)


def on_device(solution, material, neighbours, refine_count):
    return finish(step(solution, material, neighbours, refine_count))


def solution(mesh):
    in_specs = (
        P(None, ("space", "help"), None),
        P(None, ("space", "help"), None),
        P(None, ("space", "help")),
        P("space", "help"),
    )
    out_specs = P(None, ("space", "help"), None)
    return jax.shard_map(
        on_device, mesh=mesh, in_specs=in_specs, out_specs=out_specs, check_vma=False
    )
```

time: 38.9 us -> 31.4 us (0.81)
  the two profiles are of different devices: /device:TPU:29 before, /device:TPU:0 now
where the time goes in v2:
time: 31.4 us; the launch traced here: 31.2 us
  Pallas kernels  30.5 us (97%)
  between operations  0.66 us (2%)
    pallas_call x1, Pallas kernels, step(): pl.pallas_call(step_kernel, out_shape=shape(9 * NODES, CELLS), in_specs=[...  23.9 us
    pallas_call x1, Pallas kernels, finish(): pl.pallas_call(finish_kernel, out_shape=shape(9, CELLS, NODES), grid=(9,)...  6.66 us

profile of v2, /device:TPU:0, one launch (start us, length us, event | category | flops | bytes accessed | tf_op | source)
XLA Modules:
  0.0 31.2 jit_solution(402126512906761902)
XLA Ops:
  0.7 23.9 %step.1.e_ref = f32[4608,128]{1,0:T(8,128)} custom-call(f32[9,128,512]{2,1,0:T(8,128)} %sol_hbm.1, f32[3,128,512]{2,1,0:T(8,128)} %mat_hbm.1, s32[6,128]{1,0:T(8,128)} %n_hbm.1, s32[1,1]{1,0:T(1,128)S(6)} %copy.6.count_ref, f32[128,256]{1,0:T(8,128)} %constant.2.clone.k_hbm), custom_call_target="tpu_custom_call" | custom-call | tf_op jit(solution)/shard_map/step/pallas_call | solution.py:346
  24.5 6.7 %finish.1 = f32[9,128,512]{2,1,0:T(8,128)} custom-call(f32[4608,128]{1,0:T(8,128)} %step.1.e_ref), custom_call_target="tpu_custom_call" | custom-call | tf_op jit(solution)/shard_map/finish/pallas_call | solution.py:382

commit v3 on v2

--- a/solution.py
+++ b/solution.py
@@ -17,7 +17,7 @@
 LIFT = 0.5
 F32 = jnp.float32
 BF16 = jnp.bfloat16
-VMEM_LIMIT = 61 * 2**20
+VMEM_LIMIT = 32 * 2**20
 
 COLS = (6, 7, 8, 4, 3, 1, 5, 2)
 X_FIELDS = (6, 7, 8, 0, 3, 5)
@@ -150,10 +150,10 @@
 
 def step_kernel(
     sol_hbm, mat_hbm, n_hbm, count_ref, k_hbm,
-    e_hbm,
+    e_ref,
     sol_ref, mat_ref, n_ref, k_ref, q0_ref, q_ref, u_ref, i_ref, m_ref, t_ref, x_ref, far_ref,
-    e_ref, before_ref, after_ref, low_ref, high_ref,
-    sem, send_sem, recv_sem, out_sem,
+    before_ref, after_ref, low_ref, high_ref,
+    sem, send_sem, recv_sem,
 ):
     me = lax.axis_index("space")
     peers = lax.axis_size("space")
@@ -222,13 +222,6 @@
         send.start()
     volume_and_faces(i_ref, q0_ref, m_ref, n_ref, k_ref, e_ref, t_ref, x_ref, far_ref)
 
-    def writing(field, a, planes, slot):
-        at = pl.ds(field * NODES + a * PLANE, planes * PLANE)
-        return pltpu.make_async_copy(e_ref.at[at], e_hbm.at[at], out_sem.at[slot * 9 + field])
-
-    writes = [writing(field, 1, 6, 0) for field in range(9)]
-    for write in writes:
-        write.start()
     for send in sends:
         send.wait()
     for face, far_ref, a, sign in ((0, before_ref, 7, -1.0), (1, after_ref, 0, 1.0)):
@@ -238,11 +231,6 @@
         lam, shear, inverse = (plane(m_ref, slot, a) for slot in range(3))
         for f, value in enumerate(flux(own, other, lam, shear, inverse, 0, sign)):
             e_ref[pl.ds(f * NODES + a * PLANE, PLANE), :] = plane(e_ref, f, a) + value
-        for field in range(9):
-            writes.append(writing(field, a, 1, 1 + face))
-            writes[-1].start()
-    for write in writes:
-        write.wait()
 
 
 def fetch(far, targets):
@@ -326,13 +314,24 @@
             e_ref[pl.ds(f * NODES + own_place, PLANE, stride=8), :] = z_face(e_ref, f, own_place) + value
 
 
-def finish_kernel(e_ref, out_ref):
-    for tile in range(4):
-        out_ref[0, :, tile * 128 : (tile + 1) * 128] = e_ref[tile * 128 : (tile + 1) * 128, :].T
+def finish_kernel(e_ref, out_hbm, out_ref, sem):
+    copies = []
+    for field in range(9):
+        for tile in range(4):
+            block = e_ref[pl.ds(field * NODES + tile * 128, 128), :]
+            out_ref[field, :, tile * 128 : (tile + 1) * 128] = block.T
+        copies.append(pltpu.make_async_copy(out_ref.at[field], out_hbm.at[field], sem.at[field]))
+        copies[-1].start()
+    for copy in copies:
+        copy.wait()
 
 
 def shape(*dims):
     return jax.ShapeDtypeStruct(dims, F32)
+
+
+def in_hbm(value):
+    return pltpu.with_memory_space_constraint(value, pltpu.MemorySpace.HBM)
 
 
 def step(solution, material, neighbours, refine_count):
@@ -345,9 +344,9 @@
 
     return pl.pallas_call(
         step_kernel,
-        out_shape=shape(9 * NODES, CELLS),
+        out_shape=pltpu.VMEM((9 * NODES, CELLS), F32),
         in_specs=[hbm, hbm, hbm, smem, hbm],
-        out_specs=hbm,
+        out_specs=pl.BlockSpec(memory_space=pltpu.VMEM),
         scratch_shapes=[
             pltpu.VMEM((9, CELLS, NODES), F32),
             pltpu.VMEM((3, CELLS, NODES), F32),
@@ -361,7 +360,6 @@
             field_buffer(8),
             field_buffer(6),
             pltpu.VMEM((10 * PLANE, CELLS), F32),
-            field_buffer(9),
             pltpu.VMEM((10 * PLANE, CELLS), F32),
             pltpu.VMEM((10 * PLANE, CELLS), F32),
             pltpu.VMEM((10 * PLANE, CELLS), F32),
@@ -369,22 +367,21 @@
             pltpu.SemaphoreType.DMA((12,)),
             pltpu.SemaphoreType.DMA((2,)),
             pltpu.SemaphoreType.DMA((2,)),
-            pltpu.SemaphoreType.DMA((27,)),
         ],
         compiler_params=pltpu.CompilerParams(
             vmem_limit_bytes=VMEM_LIMIT, collective_id=0, has_side_effects=True
         ),
         name="step",
-    )(solution, material, neighbours, refine_count, table)
+    )(in_hbm(solution), in_hbm(material), in_hbm(neighbours), refine_count, in_hbm(table))
 
 
 def finish(nodal):
     return pl.pallas_call(
         finish_kernel,
         out_shape=shape(9, CELLS, NODES),
-        grid=(9,),
-        in_specs=[pl.BlockSpec((NODES, CELLS), lambda i: (i, 0))],
-        out_specs=pl.BlockSpec((1, CELLS, NODES), lambda i: (i, 0, 0)),
+        in_specs=[pl.BlockSpec(memory_space=pltpu.VMEM)],
+        out_specs=pl.BlockSpec(memory_space=pltpu.MemorySpace.HBM),
+        scratch_shapes=[pltpu.VMEM((9, CELLS, NODES), F32), pltpu.SemaphoreType.DMA((9,))],
         compiler_params=pltpu.CompilerParams(vmem_limit_bytes=VMEM_LIMIT),
         name="finish",
     )(nodal)

time: 31.4 us -> 25.2 us (0.80)
  Pallas kernels: 30.5 us -> 24.4 us
    pallas_call x2, Pallas kernels: 30.5 us -> 24.4 us  [the longest x1 22.8 us: step(): pl.pallas_call(step_kernel, out_shape=pltpu.VMEM((9 * NODES, CELLS), F32)...]
where the time goes in v3:
time: 25.2 us; the launch traced here: 25.1 us
  Pallas kernels  24.4 us (97%)
  between operations  0.66 us (3%)
    pallas_call x1, Pallas kernels, step(): pl.pallas_call(step_kernel, out_shape=pltpu.VMEM((9 * NODES, CELLS), F32)...  22.8 us
    pallas_call x1, Pallas kernels, finish(): pl.pallas_call(finish_kernel, out_shape=shape(9, CELLS, NODES), in_specs=...  1.61 us

profile of v3, /device:TPU:0, one launch (start us, length us, event | category | flops | bytes accessed | tf_op | source)
XLA Modules:
  0.0 25.1 jit_solution(7160711146863580574)
XLA Ops:
  0.7 22.8 %step.1.e_ref = f32[4608,128]{1,0:T(8,128)S(1)} custom-call(f32[9,128,512]{2,1,0:T(8,128)} %sol_hbm.1, f32[3,128,512]{2,1,0:T(8,128)} %mat_hbm.1, s32[6,128]{1,0:T(8,128)} %n_hbm.1, s32[1,1]{1,0:T(1,128)S(6)} %copy.6.count_ref, f32[128,256]{1,0:T(8,128)} %constant.2.clone.k_hbm), custom_call_target="tpu_custom_call" | custom-call | tf_op jit(solution)/shard_map/step/pallas_call | solution.py:345
  23.5 1.6 %finish.1 = f32[9,128,512]{2,1,0:T(8,128)} custom-call(f32[4608,128]{1,0:T(8,128)S(1)} %step.1.e_ref), custom_call_target="tpu_custom_call" | custom-call | tf_op jit(solution)/shard_map/finish/pallas_call | solution.py:379

commit v4 on v3

--- a/solution.py
+++ b/solution.py
@@ -152,7 +152,7 @@
     sol_hbm, mat_hbm, n_hbm, count_ref, k_hbm,
     e_ref,
     sol_ref, mat_ref, n_ref, k_ref, q0_ref, q_ref, u_ref, i_ref, m_ref, t_ref, x_ref, far_ref,
-    before_ref, after_ref, low_ref, high_ref,
+    sent_ref, got_ref,
     sem, send_sem, recv_sem,
 ):
     me = lax.axis_index("space")
@@ -193,6 +193,15 @@
             q_ref[at, :] = value
             u_ref[at, :] = value
 
+    pl.semaphore_wait(barrier, 2)
+    sends = [
+        remote(sent_ref.at[slot], got_ref.at[slot], send_sem.at[slot], recv_sem.at[slot], (right, left)[slot % 2])
+        for slot in range(4)
+    ]
+    for side, a in enumerate((0, 7)):
+        sent_ref[side] = compact(faces(i_ref, m_ref, a), False)
+        sends[side].start()
+
     def nested(turn, scale):
         slopes(u_ref, k_ref, t_ref, x_ref)
         for a in range(8):
@@ -209,28 +218,71 @@
             at = pl.ds(field * NODES + a * PLANE, PLANE)
             i_ref[at, :] = i_ref[at, :] + jnp.where(refined, value, 0.0)
 
-    for out_ref, a in ((low_ref, 0), (high_ref, 7)):
-        for field in range(9):
-            out_ref[pl.ds(field * PLANE, PLANE), :] = plane(i_ref, field, a)
-        out_ref[pl.ds(9 * PLANE, PLANE), :] = plane(m_ref, 3, a)
-    pl.semaphore_wait(barrier, 2)
-    sends = [
-        remote(low_ref, before_ref, send_sem.at[0], recv_sem.at[0], right),
-        remote(high_ref, after_ref, send_sem.at[1], recv_sem.at[1], left),
-    ]
-    for send in sends:
-        send.start()
+    for side, a in enumerate((0, 7)):
+        sent_ref[2 + side] = compact(faces(i_ref, m_ref, a), True)
+
+    @pl.when(lax.rem(me, 2) == 0)
+    def _():
+        sends[3].start()
+        sends[2].start()
+
+    @pl.when(lax.rem(me, 2) == 1)
+    def _():
+        sends[2].start()
+        sends[3].start()
+
     volume_and_faces(i_ref, q0_ref, m_ref, n_ref, k_ref, e_ref, t_ref, x_ref, far_ref)
 
     for send in sends:
         send.wait()
-    for face, far_ref, a, sign in ((0, before_ref, 7, -1.0), (1, after_ref, 0, 1.0)):
-        got = fetch(far_ref[...], n_ref[pl.ds(face, 1), :] & (CELLS - 1))
-        own = [plane(i_ref, f, a) for f in range(9)] + [plane(m_ref, 3, a)]
+    for face, a, sign in ((0, 7, -1.0), (1, 0, 1.0)):
+        got = fetch_compact(got_ref[face], got_ref[2 + face], n_ref[pl.ds(face, 1), :] & (CELLS - 1))
+        own = faces(i_ref, m_ref, a)
         other = [got[f * PLANE : (f + 1) * PLANE] for f in range(10)]
         lam, shear, inverse = (plane(m_ref, slot, a) for slot in range(3))
         for f, value in enumerate(flux(own, other, lam, shear, inverse, 0, sign)):
             e_ref[pl.ds(f * NODES + a * PLANE, PLANE), :] = plane(e_ref, f, a) + value
+
+
+def faces(i_ref, m_ref, a):
+    return [plane(i_ref, f, a) for f in range(9)] + [plane(m_ref, 3, a)]
+
+
+def as_bf16(mask):
+    return mask.astype(F32).astype(BF16)
+
+
+def compact(parts, first):
+    row = lax.broadcasted_iota(jnp.int32, (CELLS, CELLS), 0)
+    column = lax.broadcasted_iota(jnp.int32, (CELLS, CELLS), 1)
+    if first:
+        top, bottom = row == jnp.where(column < 64, column, -1), row == column - 64
+    else:
+        top, bottom = row == column + 64, row == jnp.where(column < 64, -1, column)
+    top, bottom = as_bf16(top), as_bf16(bottom)
+    values = halves(jnp.concatenate(parts[:5], axis=0)) + halves(jnp.concatenate(parts[5:], axis=0))
+    return jnp.dot(
+        jnp.concatenate(values, axis=1),
+        jnp.concatenate([top, top, bottom, bottom], axis=0),
+        preferred_element_type=F32,
+    )
+
+
+def fetch_compact(upper, lower, targets):
+    row = lax.broadcasted_iota(jnp.int32, (CELLS, CELLS), 0)
+    targets = jnp.broadcast_to(targets, (CELLS, CELLS))
+    in_upper = targets >= 64
+    picks = [
+        jnp.concatenate([as_bf16(row == targets - 64), as_bf16(row == jnp.where(in_upper, targets, -1))], axis=1),
+        jnp.concatenate([as_bf16(row == jnp.where(in_upper, -1, targets)), as_bf16(row == targets + 64)], axis=1),
+    ]
+    values = halves(upper) + halves(lower)
+    both = jnp.dot(
+        jnp.concatenate(values, axis=1),
+        jnp.concatenate([picks[0], picks[0], picks[1], picks[1]], axis=0),
+        preferred_element_type=F32,
+    )
+    return jnp.concatenate([both[:, :CELLS], both[:, CELLS:]], axis=0)
 
 
 def fetch(far, targets):
@@ -360,13 +412,11 @@
             field_buffer(8),
             field_buffer(6),
             pltpu.VMEM((10 * PLANE, CELLS), F32),
-            pltpu.VMEM((10 * PLANE, CELLS), F32),
-            pltpu.VMEM((10 * PLANE, CELLS), F32),
-            pltpu.VMEM((10 * PLANE, CELLS), F32),
-            pltpu.VMEM((10 * PLANE, CELLS), F32),
+            pltpu.VMEM((4, 5 * PLANE, CELLS), F32),
+            pltpu.VMEM((4, 5 * PLANE, CELLS), F32),
             pltpu.SemaphoreType.DMA((12,)),
-            pltpu.SemaphoreType.DMA((2,)),
-            pltpu.SemaphoreType.DMA((2,)),
+            pltpu.SemaphoreType.DMA((4,)),
+            pltpu.SemaphoreType.DMA((4,)),
         ],
         compiler_params=pltpu.CompilerParams(
             vmem_limit_bytes=VMEM_LIMIT, collective_id=0, has_side_effects=True

time: 25.2 us -> 24.3 us (0.964)
  Pallas kernels: 24.4 us -> 23.5 us
    pallas_call x1, Pallas kernels: 22.8 us -> 21.9 us  [step(): pl.pallas_call(step_kernel, out_shape=pltpu.VMEM((9 * NODES, CELLS), F32)...]
where the time goes in v4:
time: 24.3 us; the launch traced here: 24.2 us
  Pallas kernels  23.5 us (97%)
  between operations  0.66 us (3%)
    pallas_call x1, Pallas kernels, step(): pl.pallas_call(step_kernel, out_shape=pltpu.VMEM((9 * NODES, CELLS), F32)...  21.9 us
    pallas_call x1, Pallas kernels, finish(): pl.pallas_call(finish_kernel, out_shape=shape(9, CELLS, NODES), in_specs=...  1.61 us

profile of v4, /device:TPU:0, one launch (start us, length us, event | category | flops | bytes accessed | tf_op | source)
XLA Modules:
  0.0 24.2 jit_solution(11652045189513864451)
XLA Ops:
  0.7 21.9 %step.1.e_ref = f32[4608,128]{1,0:T(8,128)S(1)} custom-call(f32[9,128,512]{2,1,0:T(8,128)} %sol_hbm.1, f32[3,128,512]{2,1,0:T(8,128)} %mat_hbm.1, s32[6,128]{1,0:T(8,128)} %n_hbm.1, s32[1,1]{1,0:T(1,128)S(6)} %copy.6.count_ref, f32[128,256]{1,0:T(8,128)} %constant.2.clone.k_hbm), custom_call_target="tpu_custom_call" | custom-call | tf_op jit(solution)/shard_map/step/pallas_call | solution.py:397
  22.6 1.6 %finish.1 = f32[9,128,512]{2,1,0:T(8,128)} custom-call(f32[4608,128]{1,0:T(8,128)S(1)} %step.1.e_ref), custom_call_target="tpu_custom_call" | custom-call | tf_op jit(solution)/shard_map/finish/pallas_call | solution.py:429

commit v5 on v4

--- a/solution.py
+++ b/solution.py
@@ -36,8 +36,6 @@
 
 
 TABLE = cheb_table(8)
-EVEN = [[float((TABLE[i, j] + TABLE[i, 7 - j]) / 2) for j in range(4)] for i in range(4)]
-ODD = [[float((TABLE[i, j] - TABLE[i, 7 - j]) / 2) for j in range(4)] for i in range(4)]
 
 
 def plane_table():
@@ -52,21 +50,6 @@
     return STEP ** (degree + 1) / math.factorial(degree + 1)
 
 
-def line_derivative(lines):
-    plus = [lines[j] + lines[7 - j] for j in range(4)]
-    minus = [lines[j] - lines[7 - j] for j in range(4)]
-    out = [None] * 8
-    for i in range(4):
-        first = EVEN[i][0] * plus[0]
-        second = ODD[i][0] * minus[0]
-        for j in range(1, 4):
-            first = first + EVEN[i][j] * plus[j]
-            second = second + ODD[i][j] * minus[j]
-        out[i] = second + first
-        out[7 - i] = second - first
-    return out
-
-
 def plane(ref, slot, a):
     return ref[pl.ds(slot * NODES + a * PLANE, PLANE), :]
 
@@ -77,38 +60,57 @@
     return high, low
 
 
+def matmul_table(k_ref):
+    return k_ref[...].astype(BF16)[:, :192]
+
+
+def triple(value):
+    high, low = halves(value)
+    return jnp.concatenate([high, low, high], axis=0)
+
+
+def dot(left, parts):
+    return jnp.dot(left, jnp.concatenate(parts, axis=1), preferred_element_type=F32)
+
+
+def line_slopes(i, k, q_ref, x_ref):
+    for first in range(0, 6, 2):
+        parts = []
+        for field in X_FIELDS[first : first + 2]:
+            lines = [q_ref[pl.ds(field * NODES + a * PLANE + i * 8, 8), :] for a in range(8)]
+            parts.append(triple(jnp.concatenate(lines, axis=0)))
+        along_x = dot(k[:64], parts)
+        for place in range(2):
+            for a in range(8):
+                x_ref[pl.ds((first + place) * NODES + a * PLANE + i * 8, 8), :] = along_x[
+                    a * 8 : a * 8 + 8, place * CELLS : (place + 1) * CELLS
+                ]
+
+
+def plane_slopes(i, k, q_ref, t_ref):
+    split = {field: triple(plane(q_ref, field, i)) for field in COLS}
+    both = dot(k, [split[f] for f in (6, 7, 8, 4)])
+    along_y = dot(k[:64], [split[f] for f in (3, 1)])
+    along_z = dot(k[64:], [split[f] for f in (5, 2)])
+
+    def put(slot, value):
+        t_ref[pl.ds(slot * NODES + i * PLANE, PLANE), :] = value
+
+    put(0, both[:64, 128:256])
+    put(1, both[64:, 256:384])
+    put(2, both[:64, :128])
+    put(3, both[64:, 128:256] + both[:64, 256:384])
+    put(4, both[64:, :128])
+    put(5, along_y[:, :128] + along_z[:, :128])
+    put(6, along_y[:, 128:] + both[64:, 384:])
+    put(7, both[:64, 384:] + along_z[:, 128:])
+
+
 def slopes(q_ref, k_ref, t_ref, x_ref):
-    k = k_ref[...].astype(BF16)[:, :192]
-
+    k = matmul_table(k_ref)
     for i in range(8):
-        split = {}
-        for field in COLS:
-            high, low = halves(plane(q_ref, field, i))
-            split[field] = jnp.concatenate([high, low, high], axis=0)
-
-        def dot(left, fields):
-            right = jnp.concatenate([split[f] for f in fields], axis=1)
-            return jnp.dot(left, right, preferred_element_type=F32)
-
-        both = dot(k, (6, 7, 8, 4))
-        along_y = dot(k[:64], (3, 1))
-        along_z = dot(k[64:], (5, 2))
-        for slot, field in enumerate(X_FIELDS):
-            lines = [q_ref[pl.ds(field * NODES + a * PLANE + i * 8, 8), :] for a in range(8)]
-            for a, value in enumerate(line_derivative(lines)):
-                x_ref[pl.ds(slot * NODES + a * PLANE + i * 8, 8), :] = value
-
-        def put(slot, value):
-            t_ref[pl.ds(slot * NODES + i * PLANE, PLANE), :] = value
-
-        put(0, both[:64, 128:256])
-        put(1, both[64:, 256:384])
-        put(2, both[:64, :128])
-        put(3, both[64:, 128:256] + both[:64, 256:384])
-        put(4, both[64:, :128])
-        put(5, along_y[:, :128] + along_z[:, :128])
-        put(6, along_y[:, 128:] + both[64:, 384:])
-        put(7, both[:64, 384:] + along_z[:, 128:])
+        plane_slopes(i, k, q_ref, t_ref)
+        line_slopes(i, k, q_ref, x_ref)
 
 
 def elastic_plane(a, t_ref, x_ref, m_ref, scale=None):
@@ -150,7 +152,7 @@
 
 def step_kernel(
     sol_hbm, mat_hbm, n_hbm, count_ref, k_hbm,
-    e_ref,
+    e_ref, middle_ref,
     sol_ref, mat_ref, n_ref, k_ref, q0_ref, q_ref, u_ref, i_ref, m_ref, t_ref, x_ref, far_ref,
     sent_ref, got_ref,
     sem, send_sem, recv_sem,
@@ -211,13 +213,19 @@
         return scale * ((degree + 1.0) / degree)
 
     lax.fori_loop(0, ORD - 3, nested, jnp.float32(STEP / ORD))
-    slopes(u_ref, k_ref, t_ref, x_ref)
     refined = lax.broadcasted_iota(jnp.int32, (PLANE, CELLS), 1) < count_ref[0, 0]
-    for a in range(8):
+    k = matmul_table(k_ref)
+
+    def add_extra(a):
+        plane_slopes(a, k, u_ref, t_ref)
         for field, value in enumerate(elastic_plane(a, t_ref, x_ref, m_ref, weight(2))):
             at = pl.ds(field * NODES + a * PLANE, PLANE)
             i_ref[at, :] = i_ref[at, :] + jnp.where(refined, value, 0.0)
 
+    for i in range(8):
+        line_slopes(i, k, u_ref, x_ref)
+    for a in (0, 7):
+        add_extra(a)
     for side, a in enumerate((0, 7)):
         sent_ref[2 + side] = compact(faces(i_ref, m_ref, a), True)
 
@@ -231,8 +239,13 @@
         sends[2].start()
         sends[3].start()
 
+    for a in range(1, 7):
+        add_extra(a)
     volume_and_faces(i_ref, q0_ref, m_ref, n_ref, k_ref, e_ref, t_ref, x_ref, far_ref)
 
+    for field in range(9):
+        for tile in (1, 2):
+            middle_ref[field, :, (tile - 1) * 128 : tile * 128] = e_ref[pl.ds(field * NODES + tile * 128, 128), :].T
     for send in sends:
         send.wait()
     for face, a, sign in ((0, 7, -1.0), (1, 0, 1.0)):
@@ -366,14 +379,18 @@
             e_ref[pl.ds(f * NODES + own_place, PLANE, stride=8), :] = z_face(e_ref, f, own_place) + value
 
 
-def finish_kernel(e_ref, out_hbm, out_ref, sem):
-    copies = []
+def finish_kernel(e_ref, middle_ref, out_hbm, out_ref, sem):
+    def writing(source, columns, field, slot):
+        return pltpu.make_async_copy(source, out_hbm.at[field, :, columns], sem.at[slot * 9 + field])
+
+    copies = [writing(middle_ref.at[f], pl.ds(128, 256), f, 0) for f in range(9)]
+    for copy in copies:
+        copy.start()
     for field in range(9):
-        for tile in range(4):
-            block = e_ref[pl.ds(field * NODES + tile * 128, 128), :]
-            out_ref[field, :, tile * 128 : (tile + 1) * 128] = block.T
-        copies.append(pltpu.make_async_copy(out_ref.at[field], out_hbm.at[field], sem.at[field]))
-        copies[-1].start()
+        for side, tile in enumerate((0, 3)):
+            out_ref[2 * field + side] = e_ref[pl.ds(field * NODES + tile * 128, 128), :].T
+            copies.append(writing(out_ref.at[2 * field + side], pl.ds(tile * 128, 128), field, 1 + side))
+            copies[-1].start()
     for copy in copies:
         copy.wait()
 
@@ -396,9 +413,9 @@
 
     return pl.pallas_call(
         step_kernel,
-        out_shape=pltpu.VMEM((9 * NODES, CELLS), F32),
+        out_shape=(pltpu.VMEM((9 * NODES, CELLS), F32), pltpu.VMEM((9, CELLS, 256), F32)),
         in_specs=[hbm, hbm, hbm, smem, hbm],
-        out_specs=pl.BlockSpec(memory_space=pltpu.VMEM),
+        out_specs=[pl.BlockSpec(memory_space=pltpu.VMEM)] * 2,
         scratch_shapes=[
             pltpu.VMEM((9, CELLS, NODES), F32),
             pltpu.VMEM((3, CELLS, NODES), F32),
@@ -425,20 +442,20 @@
     )(in_hbm(solution), in_hbm(material), in_hbm(neighbours), refine_count, in_hbm(table))
 
 
-def finish(nodal):
+def finish(nodal, middle):
     return pl.pallas_call(
         finish_kernel,
         out_shape=shape(9, CELLS, NODES),
-        in_specs=[pl.BlockSpec(memory_space=pltpu.VMEM)],
+        in_specs=[pl.BlockSpec(memory_space=pltpu.VMEM)] * 2,
         out_specs=pl.BlockSpec(memory_space=pltpu.MemorySpace.HBM),
-        scratch_shapes=[pltpu.VMEM((9, CELLS, NODES), F32), pltpu.SemaphoreType.DMA((9,))],
+        scratch_shapes=[pltpu.VMEM((18, CELLS, 128), F32), pltpu.SemaphoreType.DMA((27,))],
         compiler_params=pltpu.CompilerParams(vmem_limit_bytes=VMEM_LIMIT),
         name="finish",
-    )(nodal)
+    )(nodal, middle)
 
 
 def on_device(solution, material, neighbours, refine_count):
-    return finish(step(solution, material, neighbours, refine_count))
+    return finish(*step(solution, material, neighbours, refine_count))
 
 
 def solution(mesh):

time: 24.3 us -> 23.7 us (0.975)
  Pallas kernels: 23.5 us -> 22.9 us
    pallas_call x1, Pallas kernels: 21.9 us -> 21.3 us  [step(): pl.pallas_call(step_kernel, out_shape=(pltpu.VMEM((9 * NODES, CELLS), F32...]
where the time goes in v5:
time: 23.7 us; the launch traced here: 23.5 us
  Pallas kernels  22.9 us (97%)
  between operations  0.66 us (3%)
    pallas_call x1, Pallas kernels, step(): pl.pallas_call(step_kernel, out_shape=(pltpu.VMEM((9 * NODES, CELLS), F32...  21.3 us
    pallas_call x1, Pallas kernels, finish(): pl.pallas_call(finish_kernel, out_shape=shape(9, CELLS, NODES), in_specs=...  1.62 us

profile of v5, /device:TPU:0, one launch (start us, length us, event | category | flops | bytes accessed | tf_op | source)
XLA Modules:
  0.0 23.5 jit_solution(8280743075363621321)
XLA Ops:
  0.7 21.3 %step.1 = (f32[4608,128]{1,0:T(8,128)S(1)}, f32[9,128,256]{2,1,0:T(8,128)S(1)}) custom-call(f32[9,128,512]{2,1,0:T(8,128)} %sol_hbm.1, f32[3,128,512]{2,1,0:T(8,128)} %mat_hbm.1, s32[6,128]{1,0:T(8,128)} %n_hbm.1, s32[1,1]{1,0:T(1,128)S(6)} %copy.6.count_ref, f32[128,256]{1,0:T(8,128)} %constant.2.clone.k_hbm), custom_call_target="tpu_custom_call" | custom-call | tf_op jit(solution)/shard_map/step/pallas_call | solution.py:414
  21.9 1.6 %finish.1 = f32[9,128,512]{2,1,0:T(8,128)} custom-call(f32[4608,128]{1,0:T(8,128)S(1)} %get-tuple-element.7.e_ref, f32[9,128,256]{2,1,0:T(8,128)S(1)} %get-tuple-element.8.middle_ref), custom_call_target="tpu_custom_call" | custom-call | tf_op jit(solution)/shard_map/finish/pallas_call | solution.py:446

commit v6 on v5

--- a/solution.py
+++ b/solution.py
@@ -88,29 +88,35 @@
 
 
 def plane_slopes(i, k, q_ref, t_ref):
-    split = {field: triple(plane(q_ref, field, i)) for field in COLS}
-    both = dot(k, [split[f] for f in (6, 7, 8, 4)])
-    along_y = dot(k[:64], [split[f] for f in (3, 1)])
-    along_z = dot(k[64:], [split[f] for f in (5, 2)])
-
     def put(slot, value):
         t_ref[pl.ds(slot * NODES + i * PLANE, PLANE), :] = value
 
-    put(0, both[:64, 128:256])
-    put(1, both[64:, 256:384])
-    put(2, both[:64, :128])
-    put(3, both[64:, 128:256] + both[:64, 256:384])
-    put(4, both[64:, :128])
+    def part(field):
+        return triple(plane(q_ref, field, i))
+
+    one = dot(k, [part(6), part(7)])
+    put(2, one[:64, :128])
+    put(4, one[64:, :128])
+    put(0, one[:64, 128:])
+    put(3, one[64:, 128:])
+    two = dot(k, [part(8), part(4)])
+    put(1, two[64:, :128])
+    put(3, plane(t_ref, 3, i) + two[:64, :128])
+    put(7, two[:64, 128:])
+    put(6, two[64:, 128:])
+    along_y = dot(k[:64], [part(3), part(1)])
+    along_z = dot(k[64:], [part(5), part(2)])
     put(5, along_y[:, :128] + along_z[:, :128])
-    put(6, along_y[:, 128:] + both[64:, 384:])
-    put(7, both[:64, 384:] + along_z[:, 128:])
+    put(6, plane(t_ref, 6, i) + along_y[:, 128:])
+    put(7, plane(t_ref, 7, i) + along_z[:, 128:])
 
 
 def slopes(q_ref, k_ref, t_ref, x_ref):
     k = matmul_table(k_ref)
     for i in range(8):
+        line_slopes(i, k, q_ref, x_ref)
+    for i in range(8):
         plane_slopes(i, k, q_ref, t_ref)
-        line_slopes(i, k, q_ref, x_ref)
 
 
 def elastic_plane(a, t_ref, x_ref, m_ref, scale=None):
@@ -224,20 +230,10 @@
 
     for i in range(8):
         line_slopes(i, k, u_ref, x_ref)
-    for a in (0, 7):
+    for side, a in enumerate((0, 7)):
         add_extra(a)
-    for side, a in enumerate((0, 7)):
         sent_ref[2 + side] = compact(faces(i_ref, m_ref, a), True)
-
-    @pl.when(lax.rem(me, 2) == 0)
-    def _():
-        sends[3].start()
-        sends[2].start()
-
-    @pl.when(lax.rem(me, 2) == 1)
-    def _():
-        sends[2].start()
-        sends[3].start()
+        sends[2 + side].start()
 
     for a in range(1, 7):
         add_extra(a)

time: 23.7 us -> 22.9 us (0.966)
  Pallas kernels: 22.9 us -> 22.1 us
    pallas_call x1, Pallas kernels: 21.3 us -> 20.5 us  [step(): pl.pallas_call(step_kernel, out_shape=(pltpu.VMEM((9 * NODES, CELLS), F32...]
where the time goes in v6:
time: 22.9 us; the launch traced here: 22.8 us
  Pallas kernels  22.1 us (97%)
  between operations  0.66 us (3%)
    pallas_call x1, Pallas kernels, step(): pl.pallas_call(step_kernel, out_shape=(pltpu.VMEM((9 * NODES, CELLS), F32...  20.5 us
    pallas_call x1, Pallas kernels, finish(): pl.pallas_call(finish_kernel, out_shape=shape(9, CELLS, NODES), in_specs=...  1.62 us

profile of v6, /device:TPU:0, one launch (start us, length us, event | category | flops | bytes accessed | tf_op | source)
XLA Modules:
  0.0 22.8 jit_solution(10740871434465504162)
XLA Ops:
  0.7 20.5 %step.1 = (f32[4608,128]{1,0:T(8,128)S(1)}, f32[9,128,256]{2,1,0:T(8,128)S(1)}) custom-call(f32[9,128,512]{2,1,0:T(8,128)} %sol_hbm.1, f32[3,128,512]{2,1,0:T(8,128)} %mat_hbm.1, s32[6,128]{1,0:T(8,128)} %n_hbm.1, s32[1,1]{1,0:T(1,128)S(6)} %copy.6.count_ref, f32[128,256]{1,0:T(8,128)} %constant.2.clone.k_hbm), custom_call_target="tpu_custom_call" | custom-call | tf_op jit(solution)/shard_map/step/pallas_call | solution.py:410
  21.2 1.6 %finish.1 = f32[9,128,512]{2,1,0:T(8,128)} custom-call(f32[4608,128]{1,0:T(8,128)S(1)} %get-tuple-element.7.e_ref, f32[9,128,256]{2,1,0:T(8,128)S(1)} %get-tuple-element.8.middle_ref), custom_call_target="tpu_custom_call" | custom-call | tf_op jit(solution)/shard_map/finish/pallas_call | solution.py:442
